TPU v7x, 32 devices: a whole 2x2x4 slice. The times are simulated.
32 devices in a mesh: groups: 2 (over y), epoch: 4 (over z), strip: 2 (over x), band: 2 (over core).
Axes of the slice: x: 2, y: 2, z: 4, core: 2. Of those that a mesh axis runs over, the one named last changes fastest.
Arguments:
- template: bfloat16 [16, 48, 512], P(('groups', 'epoch'), 'strip', 'band'), parts along dimension 0, may hold values from -6 to 6
- science: float32 [32, 48, 512], P(('groups', 'epoch'), 'strip', 'band'), parts along dimension 0, may hold values from -6 to 6
- variance: float32 [32, 48, 512], P(('groups', 'epoch'), 'strip', 'band'), parts along dimension 0, may hold values from 2 to 40
- bad_mask: int32 [32, 48, 512], P(('groups', 'epoch'), 'strip', 'band'), parts along dimension 0, may hold values 0 or 1
- intersection: int32 [32], P('groups'), parts along dimension 0, may hold values from 0 to 7, as said below
- offsets: int32 [32, 2], P(('groups', 'epoch')), parts along dimension 0, may hold values from -4 to 4
- basis_index: int32 [32, 16], P(('groups', 'epoch')), parts along dimension 0, may hold values from 0 to 48
- coefficients: float32 [32, 16, 6], P(('groups', 'epoch')), parts along dimension 0, may hold values from -2 to 2
- basis: float32 [49, 19, 19], replicated, may hold values from -0.3125 to 0.3125
Outputs:
- residual_image: float32 [32, 48, 512], P(('groups', 'epoch'), 'strip', 'band'), parts along dimension 0
- coadd: float32 [16, 48, 512], P(('groups', 'epoch'), 'strip', 'band'), parts along dimension 0
There are 2 independent parts, one for each index of `groups`. A program takes and returns all parts, laid end to end along the dimension named above; an argument that names none is the same for every part. Nothing has to cross between parts.
Inputs may be any that keep to these rules, and one draw needn't show every extreme that they name: `intersection`: exposure d * 4 + k (k < 4) covers a tile with index from (k) * 2 to (k) * 2 + 1, chosen at random among these.
All inputs are finite; a program needn't handle non-finite values. No bound on the sum of `bad_mask` on one device may be relied on, other than what follows from the above.
Results may differ from a plain program's by a relative error of at most 0.0018.
Values may be sent and summed in bfloat16 or wider, within the bound.
A program may use at most 64 MiB of HBM per device.

v0:
```python
import functools

import jax
import jax.numpy as jnp
from jax import lax
from jax.experimental import pallas as pl
from jax.experimental.pallas import tpu as pltpu
from jax.sharding import PartitionSpec as P

HALF = 9
SHIFT = 4
RIM = HALF + SHIFT
EDGE_ROWS = 16
LANES = 128
SLOT = 64

MESH = pl.DeviceIdType.MESH
STEPS = [(ds, db) for ds in (-1, 1, 0) for db in (-1, 1, 0)]


def kernel(
    sizes,
    intersection_hbm,
    offsets_hbm,
    basis_index_hbm,
    coefficients_hbm,
    template_hbm,
    science_hbm,
    variance_hbm,
    bad_mask_hbm,
    basis_hbm,
    residual_out,
    coadd_out,
    intersection,
    offsets,
    basis_index,
    coefficients,
    template,
    science,
    variance,
    bad_mask,
    basis,
    residual,
    coadd,
    full,
    bottom,
    mid,
    top,
    low,
    turned_basis,
    pairs,
    turns,
    toeplitz,
    weight,
    weight_in,
    value_out,
    value_in,
    own_value,
    local_sem,
    send_sem,
    recv_sem,
    back_send,
    back_recv,
):
    n_epoch, n_strip, n_band = sizes
    tile_dev, height, width = template.shape
    exp_dev = science.shape[0]
    n_poly, _, n_sel = coefficients.shape
    ks, _, n_basis = basis.shape
    group = lax.axis_index("groups")
    me = lax.axis_index("epoch")
    strip = lax.axis_index("strip")
    band = lax.axis_index("band")

    side = 2 * lax.div(2 * me, n_epoch) - 1

    def away(step):
        return lax.rem(me + n_epoch + side * step, n_epoch)

    def target(epoch, ds, db):
        return (group, epoch, strip + ds, band + db)

    def there(ds, db):
        sides = []
        if ds < 0:
            sides.append(strip >= -ds)
        if ds > 0:
            sides.append(strip < n_strip - ds)
        if db < 0:
            sides.append(band >= -db)
        if db > 0:
            sides.append(band < n_band - db)
        return sides

    def guarded(sides, body):
        if not sides:
            body()
        elif len(sides) == 1:
            pl.when(sides[0])(body)
        else:
            pl.when(jnp.logical_and(sides[0], sides[1]))(body)

    loads = [
        pltpu.make_async_copy(held, here, local_sem.at[i])
        for i, (held, here) in enumerate(
            (
                (basis_hbm, basis),
                (variance_hbm, variance),
                (bad_mask_hbm, bad_mask),
                (science_hbm, science),
                (intersection_hbm, intersection),
                (template_hbm, template),
                (basis_index_hbm, basis_index),
                (coefficients_hbm, coefficients),
                (offsets_hbm, offsets),
            )
        )
    ]
    for i in (4, 5, 6, 7, 0, 1, 2, 3, 8):
        loads[i].start()

    barrier = pltpu.get_barrier_semaphore()
    for ds, db in STEPS:

        def greet(ds=ds, db=db):
            for step in range(n_epoch):
                if step == 0 and ds == 0 and db == 0:
                    continue
                epoch = away(step)
                pl.semaphore_signal(
                    barrier, inc=1, device_id=target(epoch, ds, db), device_id_type=MESH
                )

        guarded(there(ds, db), greet)

    loads[4].wait()
    loads[5].wait()
    for step in range(n_epoch):
        epoch = away(step)
        tile = intersection[epoch * exp_dev + me] - me * tile_dev
        chosen = template[jnp.clip(tile, 0, tile_dev - 1)]
        full[epoch] = chosen
        wide = chosen.astype(jnp.float32)
        bottom[epoch] = wide[height - EDGE_ROWS :].astype(jnp.bfloat16)
    mid[me, :, LANES : LANES + width] = full[me]

    zero = jnp.bfloat16(0)

    @pl.when(strip == 0)
    def _():
        top[...] = jnp.full(top.shape, zero)

    @pl.when(strip == n_strip - 1)
    def _():
        low[...] = jnp.full(low.shape, zero)

    for edge, lanes in ((band == 0, slice(0, LANES)), (band == n_band - 1, slice(LANES + width, None))):

        @pl.when(edge)
        def _(lanes=lanes):
            mid[:, :, lanes] = jnp.full(mid[:, :, lanes].shape, zero)

            @pl.when(strip > 0)
            def _():
                top[:, :, lanes] = jnp.full(top[:, :, lanes].shape, zero)

            @pl.when(strip < n_strip - 1)
            def _():
                low[:, :, lanes] = jnp.full(low[:, :, lanes].shape, zero)

    partners = n_epoch
    if n_strip > 1:
        near = jnp.minimum(strip, 1) + jnp.minimum(n_strip - 1 - strip, 1)
        partners = partners * (1 + near)
    if n_band > 1:
        near = jnp.minimum(band, 1) + jnp.minimum(n_band - 1 - band, 1)
        partners = partners * (1 + near)
    pl.semaphore_wait(barrier, partners - 1)

    def piece(step, ds, db, arriving):
        other = away(step)
        held = {0: slice(0, width), 1: slice(width - LANES, width), -1: slice(0, LANES)}[db]
        lands = {
            0: slice(LANES, LANES + width),
            1: slice(0, LANES),
            -1: slice(LANES + width, 2 * LANES + width),
        }[db]
        slot = other if arriving else me
        source = full.at[other, :, held]
        dest = mid
        if ds == 1:
            source, dest = bottom.at[other, :, held], top
        if ds == -1:
            source, dest = full.at[other, 0:EDGE_ROWS, held], low
        return pltpu.make_async_remote_copy(
            src_ref=source,
            dst_ref=dest.at[slot, :, lands],
            send_sem=send_sem.at[other, ds + 1, db + 1],
            recv_sem=recv_sem.at[slot, ds + 1, db + 1],
            device_id=target(other, ds, db),
            device_id_type=MESH,
        )

    for step in list(range(1, n_epoch)) + [0]:
        for ds, db in STEPS:
            if step == 0 and ds == 0 and db == 0:
                continue
            guarded(there(ds, db), lambda step=step, ds=ds, db=db: piece(step, ds, db, False).start())

    def back(which, out, into, step, arriving):
        other = away(step)
        slot = other if arriving else me
        return pltpu.make_async_remote_copy(
            src_ref=out.at[other],
            dst_ref=into.at[slot],
            send_sem=back_send.at[which, other],
            recv_sem=back_recv.at[which, slot],
            device_id=target(other, 0, 0),
            device_id_type=MESH,
        )

    loads[1].wait()
    loads[2].wait()
    for exposure in range(exp_dev):
        weight[exposure] = bad_mask[exposure].astype(jnp.float32) / variance[exposure]

    loads[6].wait()
    loads[7].wait()
    lane = lax.broadcasted_iota(jnp.int32, (n_poly, LANES), 1)
    mixes = []
    for exposure in range(exp_dev):
        coefs = coefficients[:, exposure, :]
        mix = jnp.zeros((n_poly, LANES), jnp.float32)
        for j in range(n_sel):
            mix = mix + jnp.where(lane == basis_index[exposure, j], coefs[:, j : j + 1], 0.0)
        mixes.append(mix)
        if n_poly < 8:
            mixes.append(jnp.zeros((8 - n_poly, LANES), jnp.float32))
    mixes = jnp.concatenate(mixes, axis=0)

    n_pairs = (ks + 1) // 2
    rows_all = pairs.shape[0] // exp_dev
    turned_basis[...] = jnp.zeros(turned_basis.shape, jnp.float32)
    loads[0].wait()
    for b in range(ks):
        turned_basis[b * SLOT : b * SLOT + ks, 0:n_basis] = basis[:, b, :]

    for q in range(0, n_pairs, 2):
        some = lax.dot_general(
            mixes,
            turned_basis[q * LANES : (q + 2) * LANES, :],
            (((1,), (1,)), ((), ())),
            precision=lax.Precision.HIGHEST,
            preferred_element_type=jnp.float32,
        )
        some = some.astype(jnp.bfloat16).astype(jnp.float32)
        for half in range(2):
            for exposure in range(exp_dev):
                at = exposure * rows_all + (q + half) * n_poly
                pairs[at : at + n_poly, :] = some[
                    exposure * 8 : exposure * 8 + n_poly, half * LANES : (half + 1) * LANES
                ]

    for step in range(1, n_epoch):
        back(0, weight, weight_in, step, False).start()

    loads[8].wait()

    def build(exposure, carry):
        shift = offsets[0, exposure] + (SHIFT + EDGE_ROWS - RIM)
        every = pairs[pl.ds(pl.multiple_of(exposure * rows_all, 8), rows_all), :]
        for y in range(height):
            turns[y * rows_all : (y + 1) * rows_all, :] = pltpu.roll(every, shift + y, 1)
        for p in range(0, n_poly, 2):
            for q in range(n_pairs):
                halves = [
                    turns[pl.ds(q * n_poly + p + h, height, stride=rows_all), :]
                    for h in range(2)
                ]
                toeplitz[
                    exposure, p * height : (p + 2) * height, q * LANES : (q + 1) * LANES
                ] = jnp.concatenate(halves, axis=0).astype(jnp.bfloat16)
        return carry

    lax.fori_loop(0, exp_dev, build, 0)

    row = lax.broadcasted_iota(jnp.int32, (height, 1), 0) + strip * height
    col = lax.broadcasted_iota(jnp.int32, (1, width), 1) + band * width
    r = (2.0 * row.astype(jnp.float32) + 1.0) / (height * n_strip) - 1.0
    c = (2.0 * col.astype(jnp.float32) + 1.0) / (width * n_band) - 1.0
    r = jnp.broadcast_to(r, (height, width))
    c = jnp.broadcast_to(c, (height, width))

    def arrive(step):
        for ds, db in STEPS:
            if ds == 0 and db == 0 and step == 0:
                continue
            guarded(
                there(-ds, -db),
                lambda ds=ds, db=db: piece(step, ds, db, True).wait_recv(),
            )

    loads[3].wait()
    for step in range(n_epoch):
        k = away(step)
        arrive(step)
        slab = jnp.concatenate(
            [
                top[k].astype(jnp.float32),
                mid[k].astype(jnp.float32),
                low[k].astype(jnp.float32),
                jnp.zeros((SLOT - height - 2 * EDGE_ROWS, width + 2 * LANES), jnp.float32),
            ],
            axis=0,
        )
        total = width + 2 * LANES
        slab = pltpu.roll(slab, total - (LANES - RIM + SHIFT) - offsets[1, k], 1)
        slab = slab[:, : width + LANES].astype(jnp.bfloat16)
        conv = jnp.zeros((n_poly * height, width), jnp.float32)
        for first in range(0, ks, 4):
            columns = range(first, min(first + 4, ks))
            stacked = jnp.concatenate([slab[:, b : b + width] for b in columns], axis=0)
            conv = conv + jnp.dot(
                toeplitz[k, :, first * SLOT : (first + len(columns)) * SLOT],
                stacked,
                preferred_element_type=jnp.float32,
            )
        q = [conv[p * height : (p + 1) * height] for p in range(n_poly)]
        model = q[0] + r * (q[1] + r * q[3] + c * q[4]) + c * (q[2] + c * q[5])
        left = science[k] - model
        residual[k] = left
        pltpu.make_async_copy(residual.at[k], residual_out.at[k], local_sem.at[9 + k]).start()
        value = weight[k] * left
        if step == 0:
            own_value[...] = value
        else:
            value_out[k] = value
            back(1, value_out, value_in, step, False).start()

    numer = [None] * tile_dev
    denom = [None] * tile_dev
    for step in range(n_epoch):
        k = away(step)
        tile = intersection[k * exp_dev + me] - me * tile_dev
        if step == 0:
            upper, under = own_value[...], weight[me]
        else:
            back(0, weight, weight_in, step, True).wait_recv()
            back(1, value_out, value_in, step, True).wait_recv()
            upper = value_in[k]
            under = weight_in[k]
        for t in range(tile_dev):
            here = (tile == t).astype(jnp.float32)
            numer[t] = upper * here if step == 0 else numer[t] + upper * here
            denom[t] = under * here if step == 0 else denom[t] + under * here
    for t in range(tile_dev):
        coadd[t] = numer[t] / (denom[t] + 1.0)
    last = pltpu.make_async_copy(coadd, coadd_out, local_sem.at[9 + n_epoch])
    last.start()

    for step in range(n_epoch):
        for ds, db in STEPS:
            if step == 0 and ds == 0 and db == 0:
                continue
            guarded(
                there(ds, db),
                lambda step=step, ds=ds, db=db: piece(step, ds, db, False).wait_send(),
            )
        if step > 0:
            back(0, weight, weight_in, step, False).wait_send()
            back(1, value_out, value_in, step, False).wait_send()
        k = away(step)
        pltpu.make_async_copy(residual.at[k], residual_out.at[k], local_sem.at[9 + k]).wait()
    last.wait()


def leave(residual, coadd, residual_out, coadd_out, images, tiles, sem):
    parts = [
        (held.at[i], here.at[i], out.at[i])
        for held, here, out in ((residual, images, residual_out), (coadd, tiles, coadd_out))
        for i in range(here.shape[0])
    ]
    arrive = [
        pltpu.make_async_copy(held, here, sem.at[0, i]) for i, (held, here, _) in enumerate(parts)
    ]
    depart = [
        pltpu.make_async_copy(here, out, sem.at[1, i]) for i, (_, here, out) in enumerate(parts)
    ]
    for copy in arrive:
        copy.start()
    for i in range(len(parts)):
        arrive[i].wait()
        depart[i].start()
    for copy in depart:
        copy.wait()


def local(sizes, template, science, variance, bad_mask, intersection, offsets, basis_index, coefficients, basis):
    n_epoch = sizes[0]
    tile_dev, height, width = template.shape
    exp_dev = science.shape[0]
    assert exp_dev == n_epoch
    n_poly = coefficients.shape[2]
    ks = basis.shape[1]
    lanes_all = width + 2 * LANES
    n_pairs = (ks + 1) // 2
    rows_all = -(-n_poly * n_pairs // 8) * 8
    far = pl.BlockSpec(memory_space=pltpu.HBM)
    free = pl.BlockSpec(memory_space=pl.ANY)
    bf16, f32 = jnp.bfloat16, jnp.float32
    dma = pltpu.SemaphoreType.DMA
    offsets = offsets.T
    coefficients = coefficients.transpose(2, 0, 1)
    basis = basis.transpose(1, 2, 0)
    residual, coadd = pl.pallas_call(
        functools.partial(kernel, sizes),
        out_shape=(
            jax.ShapeDtypeStruct(science.shape, f32),
            jax.ShapeDtypeStruct(template.shape, f32),
        ),
        in_specs=[far] * 9,
        out_specs=(free, free),
        scratch_shapes=[
            pltpu.SMEM(intersection.shape, jnp.int32),
            pltpu.SMEM(offsets.shape, jnp.int32),
            pltpu.SMEM(basis_index.shape, jnp.int32),
            pltpu.VMEM(coefficients.shape, f32),
            pltpu.VMEM(template.shape, bf16),
            pltpu.VMEM(science.shape, f32),
            pltpu.VMEM(science.shape, f32),
            pltpu.VMEM(science.shape, jnp.int32),
            pltpu.VMEM(basis.shape, f32),
            pltpu.VMEM(science.shape, f32),
            pltpu.VMEM(template.shape, f32),
            pltpu.VMEM((n_epoch, height, width), bf16),
            pltpu.VMEM((n_epoch, EDGE_ROWS, width), bf16),
            pltpu.VMEM((exp_dev, height, lanes_all), bf16),
            pltpu.VMEM((exp_dev, EDGE_ROWS, lanes_all), bf16),
            pltpu.VMEM((exp_dev, EDGE_ROWS, lanes_all), bf16),
            pltpu.VMEM((n_pairs * LANES, LANES), f32),
            pltpu.VMEM((exp_dev * rows_all, LANES), f32),
            pltpu.VMEM((height * rows_all, LANES), f32),
            pltpu.VMEM((exp_dev, n_poly * height, n_pairs * LANES), bf16),
            pltpu.VMEM((exp_dev, height, width), f32),
            pltpu.VMEM((exp_dev, height, width), f32),
            pltpu.VMEM((exp_dev, height, width), f32),
            pltpu.VMEM((exp_dev, height, width), f32),
            pltpu.VMEM((height, width), f32),
            dma((10 + n_epoch,)),
            dma((n_epoch, 3, 3)),
            dma((n_epoch, 3, 3)),
            dma((2, n_epoch)),
            dma((2, n_epoch)),
        ],
        compiler_params=pltpu.CompilerParams(
            collective_id=0, has_side_effects=True
        ),
    )(
        intersection, offsets, basis_index, coefficients,
        template, science, variance, bad_mask, basis,
    )
    return pl.pallas_call(
        leave,
        out_shape=(
            jax.ShapeDtypeStruct(science.shape, f32),
            jax.ShapeDtypeStruct(template.shape, f32),
        ),
        in_specs=[free] * 2,
        out_specs=(free, free),
        scratch_shapes=[
            pltpu.VMEM(science.shape, f32),
            pltpu.VMEM(template.shape, f32),
            dma((2, exp_dev + tile_dev)),
        ],
    )(residual, coadd)


def solution(mesh):
    sizes = (mesh.shape["epoch"], mesh.shape["strip"], mesh.shape["band"])
    image = P(("groups", "epoch"), "strip", "band")
    split = ("groups", "epoch")
    in_specs = (
        image, image, image, image, P("groups"),
        P(split, None), P(split, None), P(split, None, None), P(),
    )
    return jax.shard_map(
        functools.partial(local, sizes),
        mesh=mesh,
        in_specs=in_specs,
        out_specs=(image, image),
        check_vma=False,
    )
```

profile of v0, /device:TPU:0, one launch (start us, length us, event | category | flops | bytes accessed | tf_op | source)
XLA Modules:
  0.0 19.1 jit_solution(13232621029422435990)
XLA Ops:
  0.6 17.0 %shard_map.104 = (f32[4,24,256]{2,1,0:T(8,128)}, f32[2,24,256]{2,1,0:T(8,128)}) custom-call(s32[16]{0:T(128)} %intersection_hbm.1, s32[2,4]{1,0:T(2,128)} %bitcast.5, s32[4,16]{1,0:T(4,128)} %basis_index_hbm.1, f32[6,4,16]{2,1,0:T(4,128)} %bitcast.4, bf16[2,24,256]{2,1,0:T(8,128)(2,1)} %template_hbm.1, f32[4,24,256]{2,1,0:T(8,128)} %science_hbm.1, ...), custom_call_target="tpu_custom_call" | custom-call | tf_op jit(solution)/shard_map/pallas_call | solution.py:415
  17.6 1.5 %shard_map.105 = (f32[4,24,256]{2,1,0:T(8,128)}, f32[2,24,256]{2,1,0:T(8,128)}) custom-call(f32[4,24,256]{2,1,0:T(8,128)} %get-tuple-element.4.residual, f32[2,24,256]{2,1,0:T(8,128)} %get-tuple-element.5.coadd), custom_call_target="tpu_custom_call" | custom-call | tf_op jit(solution)/shard_map/pallas_call | solution.py:462
where the time goes:
time: 19.3 us; the launch traced here: 19.1 us
  Pallas kernels  18.5 us (96%)
  between operations  0.64 us (3%)
    pallas_call x1, Pallas kernels, local(): pl.pallas_call(functools.partial(kernel, sizes), out_shape=(jax.ShapeDtyp...  17 us
    pallas_call x1, Pallas kernels, local(): pl.pallas_call(leave, out_shape=(jax.ShapeDtypeStruct(science.shape, f32)...  1.54 us

commit v1 on v0

--- a/solution.py
+++ b/solution.py
@@ -13,6 +13,7 @@
 EDGE_ROWS = 16
 LANES = 128
 SLOT = 64
+GROUPS = 4
 
 MESH = pl.DeviceIdType.MESH
 STEPS = [(ds, db) for ds in (-1, 1, 0) for db in (-1, 1, 0)]
@@ -47,9 +48,9 @@
     mid,
     top,
     low,
-    turned_basis,
-    pairs,
-    turns,
+    coefs,
+    kernels,
+    slab,
     toeplitz,
     weight,
     weight_in,
@@ -145,6 +146,7 @@
     mid[me, :, LANES : LANES + width] = full[me]
 
     zero = jnp.bfloat16(0)
+    slab[:, height + 2 * EDGE_ROWS :, :] = jnp.zeros((slab.shape[0], 8, LANES), jnp.float32)
 
     @pl.when(strip == 0)
     def _():
@@ -226,63 +228,82 @@
 
     loads[6].wait()
     loads[7].wait()
-    lane = lax.broadcasted_iota(jnp.int32, (n_poly, LANES), 1)
-    mixes = []
+    lane = lax.broadcasted_iota(jnp.int32, (8, LANES), 1)
+    sub = lax.broadcasted_iota(jnp.int32, (8, LANES), 0)
+    half = LANES // 2
+    highs, lows = [], []
     for exposure in range(exp_dev):
-        coefs = coefficients[:, exposure, :]
-        mix = jnp.zeros((n_poly, LANES), jnp.float32)
+        for p in range(n_poly):
+            coefs[exposure, p : p + 1, 0:n_sel] = coefficients[p, exposure : exposure + 1, :]
+    for exposure in range(exp_dev):
+        some = coefs[exposure]
+        parts = []
         for j in range(n_sel):
-            mix = mix + jnp.where(lane == basis_index[exposure, j], coefs[:, j : j + 1], 0.0)
-        mixes.append(mix)
-        if n_poly < 8:
-            mixes.append(jnp.zeros((8 - n_poly, LANES), jnp.float32))
-    mixes = jnp.concatenate(mixes, axis=0)
+            column = jnp.broadcast_to(some[:, j : j + 1], (8, LANES))
+            parts.append(jnp.where(lane == basis_index[exposure, j], column, 0.0))
+        while len(parts) > 1:
+            parts = [
+                parts[i] + parts[i + 1] if i + 1 < len(parts) else parts[i]
+                for i in range(0, len(parts), 2)
+            ]
+        mix = jnp.where(sub < n_poly, parts[0], 0.0)
+        mix = mix + pltpu.roll(mix, half, 1)
+        high = mix.astype(jnp.bfloat16).astype(jnp.float32)
+        highs.append(high)
+        lows.append(mix - high)
+    mixes = jnp.concatenate(highs + lows, axis=0).astype(jnp.bfloat16)
 
     n_pairs = (ks + 1) // 2
-    rows_all = pairs.shape[0] // exp_dev
-    turned_basis[...] = jnp.zeros(turned_basis.shape, jnp.float32)
     loads[0].wait()
-    for b in range(ks):
-        turned_basis[b * SLOT : b * SLOT + ks, 0:n_basis] = basis[:, b, :]
-
-    for q in range(0, n_pairs, 2):
-        some = lax.dot_general(
-            mixes,
-            turned_basis[q * LANES : (q + 2) * LANES, :],
-            (((1,), (1,)), ((), ())),
-            precision=lax.Precision.HIGHEST,
-            preferred_element_type=jnp.float32,
-        )
-        some = some.astype(jnp.bfloat16).astype(jnp.float32)
-        for half in range(2):
-            for exposure in range(exp_dev):
-                at = exposure * rows_all + (q + half) * n_poly
-                pairs[at : at + n_poly, :] = some[
-                    exposure * 8 : exposure * 8 + n_poly, half * LANES : (half + 1) * LANES
-                ]
+    blank = jnp.zeros((8, LANES), jnp.float32)
+
+    def taps(b, g):
+        if b >= ks or g * 8 >= ks:
+            return blank
+        here = min(8, ks - g * 8)
+        tile = basis[g * 8 : g * 8 + here, b, :]
+        if here < 8:
+            tile = jnp.concatenate([tile, jnp.zeros((8 - here, tile.shape[1]), jnp.float32)], axis=0)
+        tile = jnp.concatenate([tile, jnp.zeros((8, LANES - tile.shape[1]), jnp.float32)], axis=1)
+        high = tile.astype(jnp.bfloat16).astype(jnp.float32)
+        return jnp.where(lane < half, high, pltpu.roll(tile - high, half, 1))
+
+    table = jnp.concatenate(
+        [
+            taps(2 * q + h, g)
+            for q in range(n_pairs)
+            for g in range(GROUPS)
+            for h in range(2)
+        ],
+        axis=0,
+    ).astype(jnp.bfloat16)
+    both = lax.dot_general(
+        mixes, table, (((1,), (1,)), ((), ())), preferred_element_type=jnp.float32
+    )
+    mixed = both[: 8 * exp_dev] + both[8 * exp_dev :]
+    kernels[...] = mixed.astype(jnp.bfloat16).astype(jnp.float32)
 
     for step in range(1, n_epoch):
         back(0, weight, weight_in, step, False).start()
 
     loads[8].wait()
-
-    def build(exposure, carry):
-        shift = offsets[0, exposure] + (SHIFT + EDGE_ROWS - RIM)
-        every = pairs[pl.ds(pl.multiple_of(exposure * rows_all, 8), rows_all), :]
-        for y in range(height):
-            turns[y * rows_all : (y + 1) * rows_all, :] = pltpu.roll(every, shift + y, 1)
+    later = jnp.bitwise_and(lane, 7) >= sub
+    n_tiles = n_pairs * SLOT // LANES
+    for exposure in range(exp_dev):
         for p in range(0, n_poly, 2):
-            for q in range(n_pairs):
-                halves = [
-                    turns[pl.ds(q * n_poly + p + h, height, stride=rows_all), :]
-                    for h in range(2)
-                ]
+            for t in range(n_tiles):
+                halves = []
+                for h in range(2):
+                    at = exposure * 8 + p + h
+                    wide = jnp.broadcast_to(
+                        kernels[at : at + 1, t * LANES : (t + 1) * LANES], (8, LANES)
+                    )
+                    near = pltpu.roll(wide, 0, 1, stride=1, stride_axis=0)
+                    far = pltpu.roll(wide, 8, 1, stride=1, stride_axis=0)
+                    halves.append(jnp.where(later, near, far))
                 toeplitz[
-                    exposure, p * height : (p + 2) * height, q * LANES : (q + 1) * LANES
+                    exposure, p * 8 : (p + 2) * 8, t * LANES : (t + 1) * LANES
                 ] = jnp.concatenate(halves, axis=0).astype(jnp.bfloat16)
-        return carry
-
-    lax.fori_loop(0, exp_dev, build, 0)
 
     row = lax.broadcasted_iota(jnp.int32, (height, 1), 0) + strip * height
     col = lax.broadcasted_iota(jnp.int32, (1, width), 1) + band * width
@@ -304,37 +325,60 @@
     for step in range(n_epoch):
         k = away(step)
         arrive(step)
-        slab = jnp.concatenate(
-            [
-                top[k].astype(jnp.float32),
-                mid[k].astype(jnp.float32),
-                low[k].astype(jnp.float32),
-                jnp.zeros((SLOT - height - 2 * EDGE_ROWS, width + 2 * LANES), jnp.float32),
-            ],
-            axis=0,
-        )
-        total = width + 2 * LANES
-        slab = pltpu.roll(slab, total - (LANES - RIM + SHIFT) - offsets[1, k], 1)
-        slab = slab[:, : width + LANES].astype(jnp.bfloat16)
-        conv = jnp.zeros((n_poly * height, width), jnp.float32)
-        for first in range(0, ks, 4):
-            columns = range(first, min(first + 4, ks))
-            stacked = jnp.concatenate([slab[:, b : b + width] for b in columns], axis=0)
-            conv = conv + jnp.dot(
-                toeplitz[k, :, first * SLOT : (first + len(columns)) * SLOT],
-                stacked,
-                preferred_element_type=jnp.float32,
+        n_lane = width // LANES
+        for rows, held in ((0, top), (EDGE_ROWS, mid), (EDGE_ROWS + height, low)):
+            size = held.shape[1]
+            wide = held[k].astype(jnp.float32)
+            for t in range(n_lane):
+                slab[t, rows : rows + size, :] = wide[:, (t + 1) * LANES : (t + 2) * LANES]
+            edge = lax.broadcasted_iota(jnp.int32, (size, LANES), 1) < half
+            slab[n_lane, rows : rows + size, :] = jnp.where(
+                edge, wide[:, (n_lane + 1) * LANES :], wide[:, :LANES]
             )
-        q = [conv[p * height : (p + 1) * height] for p in range(n_poly)]
-        model = q[0] + r * (q[1] + r * q[3] + c * q[4]) + c * (q[2] + c * q[5])
-        left = science[k] - model
-        residual[k] = left
+        span = height + 8 * GROUPS - 8
+        down = EDGE_ROWS - HALF + offsets[0, k]
+        along = HALF - offsets[1, k]
+        at_lane = lax.broadcasted_iota(jnp.int32, (span, LANES), 1)
+        views = []
+        for h in range(2):
+            turned = [
+                pltpu.roll(slab[t, pl.ds(down, span), :], along - h, 1) for t in range(n_lane + 1)
+            ]
+            views.append(
+                jnp.concatenate(
+                    [
+                        jnp.where(at_lane < along - h, turned[t - 1], turned[t])
+                        for t in range(n_lane + 1)
+                    ],
+                    axis=1,
+                )
+            )
+        tiles = [
+            jnp.concatenate(
+                [views[0][g * 8 : g * 8 + 8], views[1][g * 8 : g * 8 + 8]], axis=0
+            ).astype(jnp.bfloat16)
+            for g in range(span // 8)
+        ]
+        moved = [[tile[:, 2 * q : 2 * q + width] for tile in tiles] for q in range(n_pairs)]
+        factor = toeplitz[k]
+        for block in range(height // 8):
+            stacked = jnp.concatenate(
+                [moved[q][block + g] for q in range(n_pairs) for g in range(GROUPS)], axis=0
+            )
+            conv = jnp.dot(factor, stacked, preferred_element_type=jnp.float32)
+            q = [conv[p * 8 : (p + 1) * 8] for p in range(n_poly)]
+            at = slice(block * 8, block * 8 + 8)
+            rr, cc = r[at], c[at]
+            model = q[0] + rr * (q[1] + rr * q[3] + cc * q[4]) + cc * (q[2] + cc * q[5])
+            left = science[k, at] - model
+            residual[k, at] = left
+            value = weight[k, at] * left
+            if step == 0:
+                own_value[at] = value
+            else:
+                value_out[k, at] = value
         pltpu.make_async_copy(residual.at[k], residual_out.at[k], local_sem.at[9 + k]).start()
-        value = weight[k] * left
-        if step == 0:
-            own_value[...] = value
-        else:
-            value_out[k] = value
+        if step > 0:
             back(1, value_out, value_in, step, False).start()
 
     numer = [None] * tile_dev
@@ -404,7 +448,6 @@
     ks = basis.shape[1]
     lanes_all = width + 2 * LANES
     n_pairs = (ks + 1) // 2
-    rows_all = -(-n_poly * n_pairs // 8) * 8
     far = pl.BlockSpec(memory_space=pltpu.HBM)
     free = pl.BlockSpec(memory_space=pl.ANY)
     bf16, f32 = jnp.bfloat16, jnp.float32
@@ -437,10 +480,10 @@
             pltpu.VMEM((exp_dev, height, lanes_all), bf16),
             pltpu.VMEM((exp_dev, EDGE_ROWS, lanes_all), bf16),
             pltpu.VMEM((exp_dev, EDGE_ROWS, lanes_all), bf16),
-            pltpu.VMEM((n_pairs * LANES, LANES), f32),
-            pltpu.VMEM((exp_dev * rows_all, LANES), f32),
-            pltpu.VMEM((height * rows_all, LANES), f32),
-            pltpu.VMEM((exp_dev, n_poly * height, n_pairs * LANES), bf16),
+            pltpu.VMEM((exp_dev, 8, LANES), f32),
+            pltpu.VMEM((8 * exp_dev, n_pairs * SLOT), f32),
+            pltpu.VMEM((width // LANES + 1, 2 * EDGE_ROWS + height + 8, LANES), f32),
+            pltpu.VMEM((exp_dev, n_poly * 8, n_pairs * SLOT), bf16),
             pltpu.VMEM((exp_dev, height, width), f32),
             pltpu.VMEM((exp_dev, height, width), f32),
             pltpu.VMEM((exp_dev, height, width), f32),

time: 19.3 us -> 18.9 us (0.979)
  Pallas kernels: 18.5 us -> 18 us
    pallas_call x1, Pallas kernels: 17 us -> 16.5 us  [local(): pl.pallas_call(functools.partial(kernel, sizes), out_shape=(jax.ShapeDtyp...]
where the time goes in v1:
time: 18.9 us; the launch traced here: 18.7 us
  Pallas kernels  18 us (95%)
  between operations  0.64 us (3%)
    pallas_call x1, Pallas kernels, local(): pl.pallas_call(functools.partial(kernel, sizes), out_shape=(jax.ShapeDtyp...  16.5 us
    pallas_call x1, Pallas kernels, local(): pl.pallas_call(leave, out_shape=(jax.ShapeDtypeStruct(science.shape, f32)...  1.54 us

profile of v1, /device:TPU:0, one launch (start us, length us, event | category | flops | bytes accessed | tf_op | source)
XLA Modules:
  0.0 18.7 jit_solution(11194339121015941270)
XLA Ops:
  0.6 16.5 %shard_map.104 = (f32[4,24,256]{2,1,0:T(8,128)}, f32[2,24,256]{2,1,0:T(8,128)}) custom-call(s32[16]{0:T(128)} %intersection_hbm.1, s32[2,4]{1,0:T(2,128)} %bitcast.5, s32[4,16]{1,0:T(4,128)} %basis_index_hbm.1, f32[6,4,16]{2,1,0:T(4,128)} %bitcast.4, bf16[2,24,256]{2,1,0:T(8,128)(2,1)} %template_hbm.1, f32[4,24,256]{2,1,0:T(8,128)} %science_hbm.1, ...), custom_call_target="tpu_custom_call" | custom-call | tf_op jit(solution)/shard_map/pallas_call | solution.py:458
  17.1 1.5 %shard_map.105 = (f32[4,24,256]{2,1,0:T(8,128)}, f32[2,24,256]{2,1,0:T(8,128)}) custom-call(f32[4,24,256]{2,1,0:T(8,128)} %get-tuple-element.4.residual, f32[2,24,256]{2,1,0:T(8,128)} %get-tuple-element.5.coadd), custom_call_target="tpu_custom_call" | custom-call | tf_op jit(solution)/shard_map/pallas_call | solution.py:505

commit v2 on v1

v2 whole, which is shorter than its diff:
```python
import functools

import jax
import jax.numpy as jnp
from jax import lax
from jax.experimental import pallas as pl
from jax.experimental.pallas import tpu as pltpu
from jax.sharding import PartitionSpec as P

HALF = 9
SHIFT = 4
EDGE_ROWS = 16
LANES = 128
SLOT = 64
GROUPS = 4
SCIENCE_TOP = 6.0
WEIGHT_TOP = 0.5
LEVELS = 65535.0

MESH = pl.DeviceIdType.MESH


def links_of(size, place):
    if size == 1:
        return []
    if size == 2:
        return [(1 - 2 * place, 0, place, None, None)]
    return [
        (-1, 0, 1, place > 0, place < size - 1),
        (1, 1, 0, place < size - 1, place > 0),
    ]


def both(first, second):
    if first is None:
        return second
    if second is None:
        return first
    return jnp.logical_and(first, second)


def guarded(side, body):
    if side is None:
        body()
    else:
        pl.when(side)(body)


def encode(science, weight):
    high = (science + SCIENCE_TOP) * (LEVELS / (2.0 * SCIENCE_TOP)) + 0.5
    low = weight * (LEVELS / WEIGHT_TOP) + 0.5
    high = jnp.clip(high, 0.0, LEVELS).astype(jnp.int32)
    low = jnp.clip(low, 0.0, LEVELS).astype(jnp.int32)
    return jnp.bitwise_or(jnp.left_shift(high, 16), low)


def decode(code):
    high = lax.shift_right_logical(code, jnp.full(code.shape, 16, jnp.int32))
    low = jnp.bitwise_and(code, 65535)
    science = high.astype(jnp.float32) * (2.0 * SCIENCE_TOP / LEVELS) - SCIENCE_TOP
    return science, low.astype(jnp.float32) * (WEIGHT_TOP / LEVELS)


def kernel(
    sizes,
    intersection_hbm,
    offsets_hbm,
    basis_index_hbm,
    coefficients_hbm,
    template_hbm,
    science_hbm,
    variance_hbm,
    bad_mask_hbm,
    basis_hbm,
    residual,
    coadd,
    intersection,
    offsets,
    offsets_in,
    basis_index,
    basis_index_in,
    coefficients,
    coefficients_in,
    template,
    science,
    variance,
    bad_mask,
    basis,
    chosen,
    chosen_edge,
    own_edge,
    centre,
    vertical,
    lateral,
    corner,
    own_vertical,
    own_lateral,
    own_corner,
    coefs,
    table,
    kernels,
    slab,
    toeplitz,
    weight,
    code,
    code_in,
    model_out,
    numer,
    denom,
    local_sem,
    send_sem,
    recv_sem,
    own_send,
    own_recv,
):
    n_epoch, n_strip, n_band = sizes
    tile_dev, height, width = template.shape
    exp_dev = science.shape[0]
    n_poly, _, n_sel = coefficients.shape
    ks, _, n_basis = basis.shape
    n_lane = width // LANES
    half = LANES // 2
    f32, bf16 = jnp.float32, jnp.bfloat16
    group = lax.axis_index("groups")
    me = lax.axis_index("epoch")
    strip = lax.axis_index("strip")
    band = lax.axis_index("band")

    ups = links_of(n_strip, strip)
    sides = links_of(n_band, band)
    none = (0, None, None, None, None)
    near = [(u, s) for u in [none] + ups for s in [none] + sides]

    def device(epoch, u, s):
        return (group, epoch, strip + u[0], band + s[0])

    loads = [
        pltpu.make_async_copy(held, here, local_sem.at[i])
        for i, (held, here) in enumerate(
            (
                (intersection_hbm, intersection),
                (template_hbm, template),
                (variance_hbm, variance),
                (bad_mask_hbm, bad_mask),
                (science_hbm, science),
                (basis_index_hbm, basis_index),
                (coefficients_hbm, coefficients),
                (basis_hbm, basis),
                (offsets_hbm, offsets),
            )
        )
    ]
    for load in loads:
        load.start()

    barrier = pltpu.get_barrier_semaphore()

    def greet(epoch, skip):
        for u, s in near:
            if skip and u is none and s is none:
                continue

            def hello(u=u, s=s):
                pl.semaphore_signal(
                    barrier, inc=1, device_id=device(epoch, u, s), device_id_type=MESH
                )

            guarded(both(u[3], s[3]), hello)

    greet(me, True)
    for step in range(n_epoch - 1, 0, -1):
        pl.when(me + step < n_epoch)(lambda step=step: greet(me + step, False))

    def count(size, place):
        if size < 3:
            return size
        return 1 + jnp.minimum(place, 1) + jnp.minimum(size - 1 - place, 1)

    partners = count(n_strip, strip) * count(n_band, band)
    pl.semaphore_wait(barrier, partners * (me + 1) - 1)

    def slot_of(sender, receiver):
        return sender - (sender > receiver).astype(jnp.int32)

    def lanes_of(s):
        if n_band == 2:
            start = (1 - band) * (width - LANES)
            return pl.ds(pl.multiple_of(start, LANES), LANES)
        return slice(0, LANES) if s[1] == 0 else slice(width - LANES, width)

    def copy(source, dest, sent, received, to):
        return pltpu.make_async_remote_copy(
            src_ref=source,
            dst_ref=dest,
            send_sem=sent,
            recv_sem=received,
            device_id=to,
            device_id_type=MESH,
        )

    n_up, n_side = len(ups), len(sides)
    images = []
    for u, s in near:
        i = 0 if u is none else 1 + ups.index(u)
        j = 0 if s is none else 1 + sides.index(s)
        images.append((u, s, i * (1 + n_side) + j))
    n_image = (1 + n_up) * (1 + n_side)
    CODE, COEF, OFFS, INDX = n_image, n_image + 1, n_image + 2, n_image + 3

    def image(epoch, u, s, kind, sender, at=None):
        source_at = epoch if at is None else at
        if u is none and s is none:
            source, dest = chosen.at[source_at], centre.at[sender]
        elif s is none:
            source, dest = chosen_edge.at[u[1], source_at], vertical.at[u[2], sender]
        elif u is none:
            source, dest = chosen.at[source_at, :, lanes_of(s)], lateral.at[s[2], sender]
        else:
            source = chosen_edge.at[u[1], source_at, :, lanes_of(s)]
            dest = corner.at[u[2], s[2], sender]
        return copy(
            source, dest, send_sem.at[kind], recv_sem.at[slot_of(sender, epoch), kind], device(epoch, u, s)
        )

    def arriving(epoch, u, s, kind):
        if u is none and s is none:
            dest = centre.at[epoch]
        elif s is none:
            dest = vertical.at[u[2], epoch]
        elif u is none:
            dest = lateral.at[s[2], epoch]
        else:
            dest = corner.at[u[2], s[2], epoch]
        return copy(dest, dest, send_sem.at[kind], recv_sem.at[slot_of(epoch, me), kind], device(epoch, u, s))

    def landing(links, place, size):
        if size == 2:
            return [(k[0], k[1], 1 - place, None, None) for k in links]
        return [(k[0], k[1], k[2], k[4], k[3]) for k in links]

    ups_in = landing(ups, strip, n_strip)
    sides_in = landing(sides, band, n_band)
    images_in = []
    for u, s, kind in images:
        a = none if u is none else ups_in[ups.index(u)]
        b = none if s is none else sides_in[sides.index(s)]
        images_in.append((a, b, kind))

    def send_image(epoch):
        for u, s, kind in images:
            guarded(
                both(u[3], s[3]), lambda u=u, s=s, kind=kind: image(epoch, u, s, kind, me).start()
            )

    def wait_image(epoch):
        for u, s, kind in images_in:
            guarded(
                both(u[3], s[3]), lambda u=u, s=s, kind=kind: arriving(epoch, u, s, kind).wait_recv()
            )

    def small(epoch, sender):
        return [
            copy(held, into.at[sender], send_sem.at[kind], recv_sem.at[slot_of(sender, epoch), kind], device(epoch, none, none))
            for held, into, kind in (
                (offsets_hbm, offsets_in, OFFS),
                (basis_index_hbm, basis_index_in, INDX),
                (coefficients_hbm, coefficients_in, COEF),
            )
        ]

    def coded(epoch, sender):
        return copy(
            code.at[epoch], code_in.at[sender], send_sem.at[CODE], recv_sem.at[slot_of(sender, epoch), CODE],
            device(epoch, none, none),
        )

    def own_piece(u, s, kind, incoming):
        if s is none:
            source, dest = own_edge.at[0 if incoming else u[1]], own_vertical.at[u[2]]
        elif u is none:
            source, dest = template.at[:, :, lanes_of(s)], own_lateral.at[s[2]]
        else:
            source = own_edge.at[0 if incoming else u[1], :, :, lanes_of(s)]
            dest = own_corner.at[u[2], s[2]]
        if incoming:
            source = dest
        return copy(source, dest, own_send.at[kind], own_recv.at[kind], device(me, u, s))

    def send_small(epoch):
        for one in small(epoch, me):
            one.start()

    for epoch in range(n_epoch - 1):
        pl.when(epoch < me)(lambda epoch=epoch: send_small(epoch))

    loads[0].wait()
    loads[1].wait()

    def rim(wide, which):
        low, high = wide[:EDGE_ROWS], wide[height - EDGE_ROWS :]
        if n_strip == 2:
            return jnp.where(strip == 0, high, low)
        return low if which == 0 else high

    for epoch in range(n_epoch):
        tile = intersection[epoch * exp_dev + me] - me * tile_dev
        picked = template[jnp.clip(tile, 0, tile_dev - 1)]
        chosen[epoch] = picked
        wide = picked.astype(f32)
        for which in range(n_up):
            chosen_edge[which, epoch] = rim(wide, which).astype(bf16)
    for epoch in range(n_epoch - 1):
        pl.when(epoch < me)(lambda epoch=epoch: send_image(epoch))
    for t in range(tile_dev):
        wide = template[t].astype(f32)
        for which in range(n_up):
            own_edge[which, t] = rim(wide, which).astype(bf16)
    for u, s, kind in images[1:]:
        guarded(both(u[3], s[3]), lambda u=u, s=s, kind=kind: own_piece(u, s, kind, False).start())

    def clear(ref):
        ref[...] = jnp.zeros(ref.shape, ref.dtype)

    def clear_up(slot):
        clear(vertical.at[slot])
        clear(own_vertical.at[slot])

    def clear_side(slot):
        clear(lateral.at[slot])
        clear(own_lateral.at[slot])

    def clear_corner(slot, at):
        clear(corner.at[slot, at])
        clear(own_corner.at[slot, at])

    loads[2].wait()
    loads[3].wait()
    loads[4].wait()
    for epoch in range(n_epoch):
        share = bad_mask[epoch].astype(f32) / variance[epoch]
        weight[epoch] = share
        code[epoch] = encode(science[epoch], share)
    for epoch in range(n_epoch - 1):
        pl.when(epoch < me)(lambda epoch=epoch: coded(epoch, me).start())

    if n_strip == 1:
        clear(vertical)
        clear(own_vertical)
        clear(corner)
        clear(own_corner)
    elif n_strip == 2:
        clear_up(strip)
        for at in range(2):
            clear_corner(strip, at)
    else:
        for slot, edge in ((0, strip == 0), (1, strip == n_strip - 1)):

            @pl.when(edge)
            def _(slot=slot):
                clear_up(slot)
                for at in range(2):
                    clear_corner(slot, at)

    if n_band == 1:
        clear(lateral)
        clear(own_lateral)
        if n_strip > 1:
            clear(corner)
            clear(own_corner)
    elif n_band == 2:
        clear_side(band)
        if n_strip == 2:
            clear_corner(1 - strip, band)
        elif n_strip > 2:
            for slot, held in ((0, strip > 0), (1, strip < n_strip - 1)):
                pl.when(held)(lambda slot=slot: clear_corner(slot, band))
    else:
        for slot, edge in ((0, band == 0), (1, band == n_band - 1)):

            @pl.when(edge)
            def _(slot=slot):
                clear_side(slot)
                for at in range(2):
                    clear_corner(at, slot)

    slab[:, :, height + 2 * EDGE_ROWS :, :] = jnp.zeros(
        (slab.shape[0], slab.shape[1], 8, LANES), f32
    )

    lane = lax.broadcasted_iota(jnp.int32, (8, LANES), 1)
    sub = lax.broadcasted_iota(jnp.int32, (8, LANES), 0)
    n_pairs = (ks + 1) // 2
    n_tiles = n_pairs * SLOT // LANES
    later = jnp.bitwise_and(lane, 7) >= sub

    def mix_of(row, coefficient, indices):
        for p in range(n_poly):
            coefs[row, p : p + 1, 0:n_sel] = coefficient(p)
        some = coefs[row]
        parts = []
        for j in range(n_sel):
            column = jnp.broadcast_to(some[:, j : j + 1], (8, LANES))
            parts.append(jnp.where(lane == indices(j), column, 0.0))
        while len(parts) > 1:
            parts = [
                parts[i] + parts[i + 1] if i + 1 < len(parts) else parts[i]
                for i in range(0, len(parts), 2)
            ]
        mix = jnp.where(sub < n_poly, parts[0], 0.0)
        mix = mix + pltpu.roll(mix, half, 1)
        high = mix.astype(bf16).astype(f32)
        return high, mix - high

    def mixed(pairs):
        rows = jnp.concatenate([p[0] for p in pairs] + [p[1] for p in pairs], axis=0)
        out = lax.dot_general(
            rows.astype(bf16), table[...], (((1,), (1,)), ((), ())), preferred_element_type=f32
        )
        size = 8 * len(pairs)
        return (out[:size] + out[size:]).astype(bf16).astype(f32)

    def spread(row, into):
        for p in range(0, n_poly, 2):
            for t in range(n_tiles):
                halves = []
                for h in range(2):
                    at = row * 8 + p + h
                    wide = jnp.broadcast_to(
                        kernels[at : at + 1, t * LANES : (t + 1) * LANES], (8, LANES)
                    )
                    close = pltpu.roll(wide, 0, 1, stride=1, stride_axis=0)
                    far = pltpu.roll(wide, 8, 1, stride=1, stride_axis=0)
                    halves.append(jnp.where(later, close, far))
                toeplitz[into, p * 8 : (p + 2) * 8, t * LANES : (t + 1) * LANES] = (
                    jnp.concatenate(halves, axis=0).astype(bf16)
                )

    loads[5].wait()
    loads[6].wait()
    pairs = [
        mix_of(
            exposure,
            lambda p, exposure=exposure: coefficients[p, exposure : exposure + 1, :],
            lambda j, exposure=exposure: basis_index[exposure, j],
        )
        for exposure in range(exp_dev)
    ]

    loads[7].wait()
    blank = jnp.zeros((8, LANES), f32)

    def taps(b, g):
        if b >= ks or g * 8 >= ks:
            return blank
        here = min(8, ks - g * 8)
        tile = basis[g * 8 : g * 8 + here, b, :]
        if here < 8:
            tile = jnp.concatenate([tile, jnp.zeros((8 - here, n_basis), f32)], axis=0)
        tile = jnp.concatenate([tile, jnp.zeros((8, LANES - n_basis), f32)], axis=1)
        high = tile.astype(bf16).astype(f32)
        return jnp.where(lane < half, high, pltpu.roll(tile - high, half, 1))

    table[...] = jnp.concatenate(
        [
            taps(2 * q + h, g)
            for q in range(n_pairs)
            for g in range(GROUPS)
            for h in range(2)
        ],
        axis=0,
    ).astype(bf16)
    kernels[0 : 8 * exp_dev] = mixed(pairs)
    loads[8].wait()
    for exposure in range(exp_dev):
        spread(exposure, exposure)

    row = lax.broadcasted_iota(jnp.int32, (height, 1), 0) + strip * height
    col = lax.broadcasted_iota(jnp.int32, (1, width), 1) + band * width
    r = (2.0 * row.astype(f32) + 1.0) / (height * n_strip) - 1.0
    c = (2.0 * col.astype(f32) + 1.0) / (width * n_band) - 1.0
    r = jnp.broadcast_to(r, (height, width))
    c = jnp.broadcast_to(c, (height, width))

    span = height + 8 * GROUPS - 8
    at_lane = lax.broadcasted_iota(jnp.int32, (span, LANES), 1)

    def lay(board, middle, up, side, edge, at):
        for rows, body, rims in (
            (0, up(0), (edge(0, 1), edge(0, 0))),
            (EDGE_ROWS, middle, (side(1), side(0))),
            (EDGE_ROWS + height, up(1), (edge(1, 1), edge(1, 0))),
        ):
            wide = body.astype(f32)
            size = wide.shape[0]
            for t in range(n_lane):
                slab[board, t, rows : rows + size, :] = wide[:, t * LANES : (t + 1) * LANES]
            first = lax.broadcasted_iota(jnp.int32, (size, LANES), 1) < half
            slab[board, n_lane, rows : rows + size, :] = jnp.where(
                first, rims[0].astype(f32), rims[1].astype(f32)
            )

    def lay_own(board, tile):
        lay(
            board,
            template[tile],
            lambda v: own_vertical[v, tile],
            lambda s: own_lateral[s, tile],
            lambda v, s: own_corner[v, s, tile],
            tile,
        )

    def lay_other(board, epoch):
        lay(
            board,
            centre[epoch],
            lambda v: vertical[v, epoch],
            lambda s: lateral[s, epoch],
            lambda v, s: corner[v, s, epoch],
            epoch,
        )

    def models(board, factor, down, along):
        views = []
        for h in range(2):
            turned = [
                pltpu.roll(slab[board, t, pl.ds(down, span), :], along - h, 1)
                for t in range(n_lane + 1)
            ]
            views.append(
                jnp.concatenate(
                    [
                        jnp.where(at_lane < along - h, turned[t - 1], turned[t])
                        for t in range(n_lane + 1)
                    ],
                    axis=1,
                )
            )
        tiles = [
            jnp.concatenate(
                [views[0][g * 8 : g * 8 + 8], views[1][g * 8 : g * 8 + 8]], axis=0
            ).astype(bf16)
            for g in range(span // 8)
        ]
        moved = [[tile[:, 2 * q : 2 * q + width] for tile in tiles] for q in range(n_pairs)]
        for block in range(height // 8):
            stacked = jnp.concatenate(
                [moved[q][block + g] for q in range(n_pairs) for g in range(GROUPS)], axis=0
            )
            conv = jnp.dot(factor, stacked, preferred_element_type=f32)
            q = [conv[p * 8 : (p + 1) * 8] for p in range(n_poly)]
            at = slice(block * 8, block * 8 + 8)
            rr, cc = r[at], c[at]
            yield at, q[0] + rr * (q[1] + rr * q[3] + cc * q[4]) + cc * (q[2] + cc * q[5])

    def tile_of(epoch):
        return intersection[epoch * exp_dev + me] - me * tile_dev

    def down_of(shift):
        return EDGE_ROWS - HALF + shift

    def along_of(shift):
        return HALF - shift

    for u, s, kind in images_in[1:]:
        guarded(both(u[3], s[3]), lambda u=u, s=s, kind=kind: own_piece(u, s, kind, True).wait_recv())

    tile = tile_of(me)
    lay_own(0, jnp.clip(tile, 0, tile_dev - 1))
    for at, model in models(0, toeplitz[me], down_of(offsets[0, me]), along_of(offsets[1, me])):
        left = science[me, at] - model
        residual[me, at] = left
        share = weight[me, at]
        for t in range(tile_dev):
            here = (tile == t).astype(f32)
            numer[t, at] = share * left * here
            denom[t, at] = share * here

    def process(step):
        ahead = me + step < n_epoch
        epoch = jnp.where(ahead, me + step, n_epoch - 1 - step)
        for one in small(me, epoch):
            one.wait_recv()
        last = exp_dev
        kernels[8 * last : 8 * last + 8] = mixed(
            [
                mix_of(
                    last,
                    lambda p: coefficients_in[epoch, p, pl.ds(me, 1), :],
                    lambda j: basis_index_in[epoch, me, j],
                )
            ]
        )
        spread(last, last)
        tile = tile_of(epoch)
        lay_own(0, jnp.clip(tile, 0, tile_dev - 1))
        for at, model in models(
            0, toeplitz[last], down_of(offsets_in[epoch, 0, me]), along_of(offsets_in[epoch, 1, me])
        ):
            model_out[at] = model

        wait_image(epoch)

        @pl.when(ahead)
        def _():
            send_image(epoch)
            send_small(epoch)
            coded(epoch, me).start()

        lay_other(1, epoch)
        for at, model in models(
            1, toeplitz[epoch], down_of(offsets[0, epoch]), along_of(offsets[1, epoch])
        ):
            residual[epoch, at] = science[epoch, at] - model

        coded(me, epoch).wait_recv()
        seen, share = decode(code_in[epoch])
        value = share * (seen - model_out[...])
        for t in range(tile_dev):
            here = (tile == t).astype(f32)
            numer[t] = numer[t] + value * here
            denom[t] = denom[t] + share * here

    if n_epoch <= 4:
        for step in range(1, n_epoch):
            process(step)
    else:
        lax.fori_loop(1, n_epoch, lambda step, carry: (process(step), carry)[1], 0)

    for t in range(tile_dev):
        coadd[t] = numer[t] / (denom[t] + 1.0)

    for u, s, kind in images[1:]:
        guarded(both(u[3], s[3]), lambda u=u, s=s, kind=kind: own_piece(u, s, kind, False).wait_send())
    if n_epoch > 1:
        rest = pl.ds(0, n_epoch - 1)
        for u, s, kind in images:

            def gone(u=u, s=s, kind=kind):
                if u is none and s is none:
                    source = chosen.at[rest]
                elif s is none:
                    source = chosen_edge.at[u[1], rest]
                elif u is none:
                    source = chosen.at[rest, :, lanes_of(s)]
                else:
                    source = chosen_edge.at[u[1], rest, :, lanes_of(s)]
                copy(source, source, send_sem.at[kind], recv_sem.at[0, kind], device(me, u, s)).wait_send()

            guarded(both(u[3], s[3]), gone)
        for held, kind in (
            (offsets_in, OFFS),
            (basis_index_in, INDX),
            (coefficients_in, COEF),
            (code, CODE),
        ):
            source = held.at[rest]
            copy(
                source, source, send_sem.at[kind], recv_sem.at[0, kind], device(me, none, none)
            ).wait_send()


def leave(residual, coadd, residual_out, coadd_out, sem):
    parts = [
        (held.at[i], out.at[i])
        for held, out in ((residual, residual_out), (coadd, coadd_out))
        for i in range(held.shape[0])
    ]
    copies = [pltpu.make_async_copy(held, out, sem.at[i]) for i, (held, out) in enumerate(parts)]
    for one in copies:
        one.start()
    for one in copies:
        one.wait()


def local(sizes, template, science, variance, bad_mask, intersection, offsets, basis_index, coefficients, basis):
    n_epoch, n_strip, n_band = sizes
    tile_dev, height, width = template.shape
    exp_dev = science.shape[0]
    assert exp_dev == n_epoch
    n_poly = coefficients.shape[2]
    n_sel = basis_index.shape[1]
    ks = basis.shape[1]
    n_pairs = (ks + 1) // 2
    far = pl.BlockSpec(memory_space=pltpu.HBM)
    near = pl.BlockSpec(memory_space=pltpu.VMEM)
    free = pl.BlockSpec(memory_space=pl.ANY)
    bf16, f32 = jnp.bfloat16, jnp.float32
    dma = pltpu.SemaphoreType.DMA
    offsets = offsets.T
    coefficients = coefficients.transpose(2, 0, 1)
    basis = basis.transpose(1, 2, 0)
    n_up, n_side = min(n_strip - 1, 2), min(n_band - 1, 2)
    n_image = (1 + n_up) * (1 + n_side)
    edges = max(n_up, 1)
    rim = EDGE_ROWS
    residual, coadd = pl.pallas_call(
        functools.partial(kernel, sizes),
        out_shape=(
            pltpu.VMEM(science.shape, f32),
            pltpu.VMEM(template.shape, f32),
        ),
        in_specs=[far] * 9,
        out_specs=(near, near),
        scratch_shapes=[
            pltpu.SMEM(intersection.shape, jnp.int32),
            pltpu.SMEM(offsets.shape, jnp.int32),
            pltpu.SMEM((n_epoch,) + offsets.shape, jnp.int32),
            pltpu.SMEM(basis_index.shape, jnp.int32),
            pltpu.SMEM((n_epoch,) + basis_index.shape, jnp.int32),
            pltpu.VMEM(coefficients.shape, f32),
            pltpu.VMEM((n_epoch,) + coefficients.shape, f32),
            pltpu.VMEM(template.shape, bf16),
            pltpu.VMEM(science.shape, f32),
            pltpu.VMEM(science.shape, f32),
            pltpu.VMEM(science.shape, jnp.int32),
            pltpu.VMEM(basis.shape, f32),
            pltpu.VMEM((n_epoch, height, width), bf16),
            pltpu.VMEM((edges, n_epoch, rim, width), bf16),
            pltpu.VMEM((edges, tile_dev, rim, width), bf16),
            pltpu.VMEM((n_epoch, height, width), bf16),
            pltpu.VMEM((2, n_epoch, rim, width), bf16),
            pltpu.VMEM((2, n_epoch, height, LANES), bf16),
            pltpu.VMEM((2, 2, n_epoch, rim, LANES), bf16),
            pltpu.VMEM((2, tile_dev, rim, width), bf16),
            pltpu.VMEM((2, tile_dev, height, LANES), bf16),
            pltpu.VMEM((2, 2, tile_dev, rim, LANES), bf16),
            pltpu.VMEM((exp_dev + 1, 8, LANES), f32),
            pltpu.VMEM((n_pairs * SLOT, LANES), bf16),
            pltpu.VMEM((8 * exp_dev + 8, n_pairs * SLOT), f32),
            pltpu.VMEM((2, width // LANES + 1, 2 * rim + height + 8, LANES), f32),
            pltpu.VMEM((exp_dev + 1, n_poly * 8, n_pairs * SLOT), bf16),
            pltpu.VMEM((exp_dev, height, width), f32),
            pltpu.VMEM((n_epoch, height, width), jnp.int32),
            pltpu.VMEM((n_epoch, height, width), jnp.int32),
            pltpu.VMEM((height, width), f32),
            pltpu.VMEM(template.shape, f32),
            pltpu.VMEM(template.shape, f32),
            dma((9,)),
            dma((n_image + 4,)),
            dma((max(n_epoch - 1, 1), n_image + 4)),
            dma((n_image,)),
            dma((n_image,)),
        ],
        compiler_params=pltpu.CompilerParams(
            collective_id=0, has_side_effects=True
        ),
    )(
        intersection, offsets, basis_index, coefficients,
        template, science, variance, bad_mask, basis,
    )
    return pl.pallas_call(
        leave,
        out_shape=(
            jax.ShapeDtypeStruct(science.shape, f32),
            jax.ShapeDtypeStruct(template.shape, f32),
        ),
        in_specs=[near] * 2,
        out_specs=(free, free),
        scratch_shapes=[dma((exp_dev + tile_dev,))],
    )(*(pltpu.with_memory_space_constraint(x, pltpu.VMEM) for x in (residual, coadd)))


def solution(mesh):
    sizes = (mesh.shape["epoch"], mesh.shape["strip"], mesh.shape["band"])
    image = P(("groups", "epoch"), "strip", "band")
    split = ("groups", "epoch")
    in_specs = (
        image, image, image, image, P("groups"),
        P(split, None), P(split, None), P(split, None, None), P(),
    )
    return jax.shard_map(
        functools.partial(local, sizes),
        mesh=mesh,
        in_specs=in_specs,
        out_specs=(image, image),
        check_vma=False,
    )
```

time: 18.9 us -> 20.9 us (1.11)
  the two profiles are of different devices: /device:TPU:0 before, /device:TPU:31 now
where the time goes in v2:
time: 20.9 us; the launch traced here: 20.7 us
  Pallas kernels  20.1 us (96%)
  between operations  0.64 us (3%)
    pallas_call x1, Pallas kernels, local(): pl.pallas_call(functools.partial(kernel, sizes), out_shape=(pltpu.VMEM(sc...  19.4 us
    pallas_call x1, Pallas kernels, local(): pl.pallas_call(leave, out_shape=(jax.ShapeDtypeStruct(science.shape, f32)...  0.7 us

profile of v2, /device:TPU:31, one launch (start us, length us, event | category | flops | bytes accessed | tf_op | source)
XLA Modules:
  0.0 20.7 jit_solution(7620602325065377828)
XLA Ops:
  0.6 19.4 %shard_map.104 = (f32[4,24,256]{2,1,0:T(8,128)S(1)}, f32[2,24,256]{2,1,0:T(8,128)S(1)}) custom-call(s32[16]{0:T(128)} %intersection_hbm.1, s32[2,4]{1,0:T(2,128)} %bitcast.5, s32[4,16]{1,0:T(4,128)} %basis_index_hbm.1, f32[6,4,16]{2,1,0:T(4,128)} %bitcast.4, bf16[2,24,256]{2,1,0:T(8,128)(2,1)} %template_hbm.1, f32[4,24,256]{2,1,0:T(8,128)} %science_hbm.1, ...), custom_call_target="tpu_custom_call" | custom-call | tf_op jit(solution)/shard_map/pallas_call | solution.py:696
  20.0 0.7 %shard_map.105 = (f32[4,24,256]{2,1,0:T(8,128)}, f32[2,24,256]{2,1,0:T(8,128)}) custom-call(f32[4,24,256]{2,1,0:T(8,128)S(1)} %get-tuple-element.4.residual, f32[2,24,256]{2,1,0:T(8,128)S(1)} %get-tuple-element.5.coadd), custom_call_target="tpu_custom_call" | custom-call | tf_op jit(solution)/shard_map/pallas_call | solution.py:751

commit v3 on v2

--- a/solution.py
+++ b/solution.py
@@ -80,7 +80,7 @@
     basis_index,
     basis_index_in,
     coefficients,
-    coefficients_in,
+    coefs_in,
     template,
     science,
     variance,
@@ -112,6 +112,7 @@
     recv_sem,
     own_send,
     own_recv,
+    token,
 ):
     n_epoch, n_strip, n_band = sizes
     tile_dev, height, width = template.shape
@@ -143,8 +144,8 @@
                 (variance_hbm, variance),
                 (bad_mask_hbm, bad_mask),
                 (science_hbm, science),
+                (coefficients_hbm, coefficients),
                 (basis_index_hbm, basis_index),
-                (coefficients_hbm, coefficients),
                 (basis_hbm, basis),
                 (offsets_hbm, offsets),
             )
@@ -152,32 +153,53 @@
     ]
     for load in loads:
         load.start()
-
-    barrier = pltpu.get_barrier_semaphore()
-
-    def greet(epoch, skip):
-        for u, s in near:
-            if skip and u is none and s is none:
-                continue
-
-            def hello(u=u, s=s):
-                pl.semaphore_signal(
-                    barrier, inc=1, device_id=device(epoch, u, s), device_id_type=MESH
-                )
-
-            guarded(both(u[3], s[3]), hello)
-
-    greet(me, True)
-    for step in range(n_epoch - 1, 0, -1):
-        pl.when(me + step < n_epoch)(lambda step=step: greet(me + step, False))
 
     def count(size, place):
         if size < 3:
             return size
         return 1 + jnp.minimum(place, 1) + jnp.minimum(size - 1 - place, 1)
 
-    partners = count(n_strip, strip) * count(n_band, band)
-    pl.semaphore_wait(barrier, partners * (me + 1) - 1)
+    def before(size, place):
+        return place if size < 3 else jnp.minimum(place, 1)
+
+    across = count(n_band, band)
+    partners = count(n_strip, strip) * across
+    ahead_of_me = before(n_strip, strip) * across + before(n_band, band)
+
+    def lower(u, s):
+        if u is not none:
+            return strip + u[0] < strip
+        return band + s[0] < band
+
+    barrier = pltpu.get_barrier_semaphore()
+
+    def signal(sem, epoch, u, s):
+        pl.semaphore_signal(sem, inc=1, device_id=device(epoch, u, s), device_id_type=MESH)
+
+    def to_epoch(sem, epoch):
+        for u, s in near:
+            guarded(both(u[3], s[3]), lambda u=u, s=s: signal(sem, epoch, u, s))
+
+    for u, s in near[1:]:
+        guarded(
+            both(both(u[3], s[3]), jnp.logical_not(lower(u, s))),
+            lambda u=u, s=s: signal(barrier, me, u, s),
+        )
+    for step in range(1, n_epoch):
+        pl.when(me + step < n_epoch)(lambda step=step: to_epoch(barrier, me + step))
+    met = partners * me + ahead_of_me
+
+    @pl.when(met > 0)
+    def _():
+        pl.semaphore_wait(barrier, met)
+
+    for u, s in near[1:]:
+        guarded(
+            both(both(u[3], s[3]), lower(u, s)),
+            lambda u=u, s=s: signal(token.at[me], me, u, s),
+        )
+    for epoch in range(n_epoch - 1):
+        pl.when(epoch < me)(lambda epoch=epoch: to_epoch(token.at[me], epoch))
 
     def slot_of(sender, receiver):
         return sender - (sender > receiver).astype(jnp.int32)
@@ -264,9 +286,14 @@
             for held, into, kind in (
                 (offsets_hbm, offsets_in, OFFS),
                 (basis_index_hbm, basis_index_in, INDX),
-                (coefficients_hbm, coefficients_in, COEF),
             )
         ]
+
+    def coefficient_tile(epoch, sender):
+        return copy(
+            coefs.at[epoch], coefs_in.at[sender], send_sem.at[COEF], recv_sem.at[slot_of(sender, epoch), COEF],
+            device(epoch, none, none),
+        )
 
     def coded(epoch, sender):
         return copy(
@@ -309,30 +336,18 @@
         wide = picked.astype(f32)
         for which in range(n_up):
             chosen_edge[which, epoch] = rim(wide, which).astype(bf16)
+    loads[5].wait()
+    for exposure in range(exp_dev):
+        coefs[exposure] = jnp.zeros((8, LANES), f32)
+        for p in range(n_poly):
+            coefs[exposure, p : p + 1, 0:n_sel] = coefficients[p, exposure : exposure + 1, :]
+
+    def send_early(epoch):
+        coefficient_tile(epoch, me).start()
+        send_image(epoch)
+
     for epoch in range(n_epoch - 1):
-        pl.when(epoch < me)(lambda epoch=epoch: send_image(epoch))
-    for t in range(tile_dev):
-        wide = template[t].astype(f32)
-        for which in range(n_up):
-            own_edge[which, t] = rim(wide, which).astype(bf16)
-    for u, s, kind in images[1:]:
-        guarded(both(u[3], s[3]), lambda u=u, s=s, kind=kind: own_piece(u, s, kind, False).start())
-
-    def clear(ref):
-        ref[...] = jnp.zeros(ref.shape, ref.dtype)
-
-    def clear_up(slot):
-        clear(vertical.at[slot])
-        clear(own_vertical.at[slot])
-
-    def clear_side(slot):
-        clear(lateral.at[slot])
-        clear(own_lateral.at[slot])
-
-    def clear_corner(slot, at):
-        clear(corner.at[slot, at])
-        clear(own_corner.at[slot, at])
-
+        pl.when(epoch < me)(lambda epoch=epoch: send_early(epoch))
     loads[2].wait()
     loads[3].wait()
     loads[4].wait()
@@ -342,6 +357,31 @@
         code[epoch] = encode(science[epoch], share)
     for epoch in range(n_epoch - 1):
         pl.when(epoch < me)(lambda epoch=epoch: coded(epoch, me).start())
+
+    for t in range(tile_dev):
+        wide = template[t].astype(f32)
+        for which in range(n_up):
+            own_edge[which, t] = rim(wide, which).astype(bf16)
+    for u, s, kind in images[1:]:
+        guarded(
+            both(both(u[3], s[3]), lower(u, s)),
+            lambda u=u, s=s, kind=kind: own_piece(u, s, kind, False).start(),
+        )
+
+    def clear(ref):
+        ref[...] = jnp.zeros(ref.shape, ref.dtype)
+
+    def clear_up(slot):
+        clear(vertical.at[slot])
+        clear(own_vertical.at[slot])
+
+    def clear_side(slot):
+        clear(lateral.at[slot])
+        clear(own_lateral.at[slot])
+
+    def clear_corner(slot, at):
+        clear(corner.at[slot, at])
+        clear(own_corner.at[slot, at])
 
     if n_strip == 1:
         clear(vertical)
@@ -393,10 +433,7 @@
     n_tiles = n_pairs * SLOT // LANES
     later = jnp.bitwise_and(lane, 7) >= sub
 
-    def mix_of(row, coefficient, indices):
-        for p in range(n_poly):
-            coefs[row, p : p + 1, 0:n_sel] = coefficient(p)
-        some = coefs[row]
+    def mix_of(some, indices):
         parts = []
         for j in range(n_sel):
             column = jnp.broadcast_to(some[:, j : j + 1], (8, LANES))
@@ -435,12 +472,10 @@
                     jnp.concatenate(halves, axis=0).astype(bf16)
                 )
 
-    loads[5].wait()
     loads[6].wait()
     pairs = [
         mix_of(
-            exposure,
-            lambda p, exposure=exposure: coefficients[p, exposure : exposure + 1, :],
+            coefs[exposure],
             lambda j, exposure=exposure: basis_index[exposure, j],
         )
         for exposure in range(exp_dev)
@@ -561,6 +596,26 @@
     def along_of(shift):
         return HALF - shift
 
+    behind = partners - 1 - ahead_of_me
+
+    @pl.when(behind > 0)
+    def _():
+        pl.semaphore_wait(token.at[me], behind)
+
+    for u, s, kind in images[1:]:
+        guarded(
+            both(both(u[3], s[3]), jnp.logical_not(lower(u, s))),
+            lambda u=u, s=s, kind=kind: own_piece(u, s, kind, False).start(),
+        )
+    for step in range(1, n_epoch):
+
+        @pl.when(me + step < n_epoch)
+        def _(epoch=me + step):
+            pl.semaphore_wait(token.at[epoch], partners)
+            send_small(epoch)
+            send_early(epoch)
+            coded(epoch, me).start()
+
     for u, s, kind in images_in[1:]:
         guarded(both(u[3], s[3]), lambda u=u, s=s, kind=kind: own_piece(u, s, kind, True).wait_recv())
 
@@ -575,19 +630,17 @@
             numer[t, at] = share * left * here
             denom[t, at] = share * here
 
+    def partner(step):
+        return jnp.where(me + step < n_epoch, me + step, n_epoch - 1 - step)
+
     def process(step):
-        ahead = me + step < n_epoch
-        epoch = jnp.where(ahead, me + step, n_epoch - 1 - step)
-        for one in small(me, epoch):
+        epoch = partner(step)
+        for one in small(me, epoch) + [coefficient_tile(me, epoch)]:
             one.wait_recv()
         last = exp_dev
         kernels[8 * last : 8 * last + 8] = mixed(
             [
-                mix_of(
-                    last,
-                    lambda p: coefficients_in[epoch, p, pl.ds(me, 1), :],
-                    lambda j: basis_index_in[epoch, me, j],
-                )
+                mix_of(coefs_in[epoch], lambda j: basis_index_in[epoch, me, j])
             ]
         )
         spread(last, last)
@@ -596,15 +649,9 @@
         for at, model in models(
             0, toeplitz[last], down_of(offsets_in[epoch, 0, me]), along_of(offsets_in[epoch, 1, me])
         ):
-            model_out[at] = model
+            model_out[epoch, at] = model
 
         wait_image(epoch)
-
-        @pl.when(ahead)
-        def _():
-            send_image(epoch)
-            send_small(epoch)
-            coded(epoch, me).start()
 
         lay_other(1, epoch)
         for at, model in models(
@@ -612,9 +659,12 @@
         ):
             residual[epoch, at] = science[epoch, at] - model
 
+    def gather(step):
+        epoch = partner(step)
+        tile = tile_of(epoch)
         coded(me, epoch).wait_recv()
         seen, share = decode(code_in[epoch])
-        value = share * (seen - model_out[...])
+        value = share * (seen - model_out[epoch])
         for t in range(tile_dev):
             here = (tile == t).astype(f32)
             numer[t] = numer[t] + value * here
@@ -623,8 +673,11 @@
     if n_epoch <= 4:
         for step in range(1, n_epoch):
             process(step)
+        for step in range(1, n_epoch):
+            gather(step)
     else:
         lax.fori_loop(1, n_epoch, lambda step, carry: (process(step), carry)[1], 0)
+        lax.fori_loop(1, n_epoch, lambda step, carry: (gather(step), carry)[1], 0)
 
     for t in range(tile_dev):
         coadd[t] = numer[t] / (denom[t] + 1.0)
@@ -650,7 +703,7 @@
         for held, kind in (
             (offsets_in, OFFS),
             (basis_index_in, INDX),
-            (coefficients_in, COEF),
+            (coefs, COEF),
             (code, CODE),
         ):
             source = held.at[rest]
@@ -708,7 +761,7 @@
             pltpu.SMEM(basis_index.shape, jnp.int32),
             pltpu.SMEM((n_epoch,) + basis_index.shape, jnp.int32),
             pltpu.VMEM(coefficients.shape, f32),
-            pltpu.VMEM((n_epoch,) + coefficients.shape, f32),
+            pltpu.VMEM((n_epoch, 8, LANES), f32),
             pltpu.VMEM(template.shape, bf16),
             pltpu.VMEM(science.shape, f32),
             pltpu.VMEM(science.shape, f32),
@@ -724,7 +777,7 @@
             pltpu.VMEM((2, tile_dev, rim, width), bf16),
             pltpu.VMEM((2, tile_dev, height, LANES), bf16),
             pltpu.VMEM((2, 2, tile_dev, rim, LANES), bf16),
-            pltpu.VMEM((exp_dev + 1, 8, LANES), f32),
+            pltpu.VMEM((exp_dev, 8, LANES), f32),
             pltpu.VMEM((n_pairs * SLOT, LANES), bf16),
             pltpu.VMEM((8 * exp_dev + 8, n_pairs * SLOT), f32),
             pltpu.VMEM((2, width // LANES + 1, 2 * rim + height + 8, LANES), f32),
@@ -732,7 +785,7 @@
             pltpu.VMEM((exp_dev, height, width), f32),
             pltpu.VMEM((n_epoch, height, width), jnp.int32),
             pltpu.VMEM((n_epoch, height, width), jnp.int32),
-            pltpu.VMEM((height, width), f32),
+            pltpu.VMEM((n_epoch, height, width), f32),
             pltpu.VMEM(template.shape, f32),
             pltpu.VMEM(template.shape, f32),
             dma((9,)),
@@ -740,6 +793,7 @@
             dma((max(n_epoch - 1, 1), n_image + 4)),
             dma((n_image,)),
             dma((n_image,)),
+            pltpu.SemaphoreType.REGULAR((n_epoch,)),
         ],
         compiler_params=pltpu.CompilerParams(
             collective_id=0, has_side_effects=True

time: 20.9 us -> 14.6 us (0.70)
  the two profiles are of different devices: /device:TPU:31 before, /device:TPU:25 now
where the time goes in v3:
time: 14.6 us; the launch traced here: 14.4 us
  Pallas kernels  13.8 us (95%)
  between operations  0.64 us (4%)
    pallas_call x1, Pallas kernels, local(): pl.pallas_call(functools.partial(kernel, sizes), out_shape=(pltpu.VMEM(sc...  13.1 us
    pallas_call x1, Pallas kernels, local(): pl.pallas_call(leave, out_shape=(jax.ShapeDtypeStruct(science.shape, f32)...  0.7 us

profile of v3, /device:TPU:25, one launch (start us, length us, event | category | flops | bytes accessed | tf_op | source)
XLA Modules:
  0.0 14.4 jit_solution(101263484596311360)
XLA Ops:
  0.6 13.1 %shard_map.104 = (f32[4,24,256]{2,1,0:T(8,128)S(1)}, f32[2,24,256]{2,1,0:T(8,128)S(1)}) custom-call(s32[16]{0:T(128)} %intersection_hbm.1, s32[2,4]{1,0:T(2,128)} %bitcast.5, s32[4,16]{1,0:T(4,128)} %basis_index_hbm.1, f32[6,4,16]{2,1,0:T(4,128)} %bitcast.4, bf16[2,24,256]{2,1,0:T(8,128)(2,1)} %template_hbm.1, f32[4,24,256]{2,1,0:T(8,128)} %science_hbm.1, ...), custom_call_target="tpu_custom_call" | custom-call | tf_op jit(solution)/shard_map/pallas_call | solution.py:749
  13.7 0.7 %shard_map.105 = (f32[4,24,256]{2,1,0:T(8,128)}, f32[2,24,256]{2,1,0:T(8,128)}) custom-call(f32[4,24,256]{2,1,0:T(8,128)S(1)} %get-tuple-element.4.residual, f32[2,24,256]{2,1,0:T(8,128)S(1)} %get-tuple-element.5.coadd), custom_call_target="tpu_custom_call" | custom-call | tf_op jit(solution)/shard_map/pallas_call | solution.py:805

commit v4 on v3

--- a/solution.py
+++ b/solution.py
@@ -131,6 +131,7 @@
     sides = links_of(n_band, band)
     none = (0, None, None, None, None)
     near = [(u, s) for u in [none] + ups for s in [none] + sides]
+    column = [(u, none) for u in [none] + ups]
 
     def device(epoch, u, s):
         return (group, epoch, strip + u[0], band + s[0])
@@ -163,7 +164,7 @@
         return place if size < 3 else jnp.minimum(place, 1)
 
     across = count(n_band, band)
-    partners = count(n_strip, strip) * across
+    partners = count(n_strip, strip)
     ahead_of_me = before(n_strip, strip) * across + before(n_band, band)
 
     def lower(u, s):
@@ -177,8 +178,8 @@
         pl.semaphore_signal(sem, inc=1, device_id=device(epoch, u, s), device_id_type=MESH)
 
     def to_epoch(sem, epoch):
-        for u, s in near:
-            guarded(both(u[3], s[3]), lambda u=u, s=s: signal(sem, epoch, u, s))
+        for u, s in column:
+            guarded(u[3], lambda u=u, s=s: signal(sem, epoch, u, s))
 
     for u, s in near[1:]:
         guarded(
@@ -229,32 +230,6 @@
     n_image = (1 + n_up) * (1 + n_side)
     CODE, COEF, OFFS, INDX = n_image, n_image + 1, n_image + 2, n_image + 3
 
-    def image(epoch, u, s, kind, sender, at=None):
-        source_at = epoch if at is None else at
-        if u is none and s is none:
-            source, dest = chosen.at[source_at], centre.at[sender]
-        elif s is none:
-            source, dest = chosen_edge.at[u[1], source_at], vertical.at[u[2], sender]
-        elif u is none:
-            source, dest = chosen.at[source_at, :, lanes_of(s)], lateral.at[s[2], sender]
-        else:
-            source = chosen_edge.at[u[1], source_at, :, lanes_of(s)]
-            dest = corner.at[u[2], s[2], sender]
-        return copy(
-            source, dest, send_sem.at[kind], recv_sem.at[slot_of(sender, epoch), kind], device(epoch, u, s)
-        )
-
-    def arriving(epoch, u, s, kind):
-        if u is none and s is none:
-            dest = centre.at[epoch]
-        elif s is none:
-            dest = vertical.at[u[2], epoch]
-        elif u is none:
-            dest = lateral.at[s[2], epoch]
-        else:
-            dest = corner.at[u[2], s[2], epoch]
-        return copy(dest, dest, send_sem.at[kind], recv_sem.at[slot_of(epoch, me), kind], device(epoch, u, s))
-
     def landing(links, place, size):
         if size == 2:
             return [(k[0], k[1], 1 - place, None, None) for k in links]
@@ -268,17 +243,48 @@
         b = none if s is none else sides_in[sides.index(s)]
         images_in.append((a, b, kind))
 
+    def landed(epoch, u, s):
+        if u is none and s is none:
+            return centre.at[epoch]
+        if s is none:
+            return vertical.at[u[2], epoch]
+        if u is none:
+            return lateral.at[s[2], epoch]
+        return corner.at[u[2], s[2], epoch]
+
     def send_image(epoch):
         for u, s, kind in images:
-            guarded(
-                both(u[3], s[3]), lambda u=u, s=s, kind=kind: image(epoch, u, s, kind, me).start()
+            if s is not none:
+                continue
+            source = chosen.at[epoch] if u is none else chosen_edge.at[u[1], epoch]
+            one = copy(
+                source, landed(me, u, s), send_sem.at[kind], recv_sem.at[slot_of(me, epoch), kind],
+                device(epoch, u, s),
             )
-
-    def wait_image(epoch):
+            guarded(u[3], one.start)
+
+    def wait_pieces(epoch, side):
         for u, s, kind in images_in:
-            guarded(
-                both(u[3], s[3]), lambda u=u, s=s, kind=kind: arriving(epoch, u, s, kind).wait_recv()
+            if (s is not none) != side:
+                continue
+            here = landed(epoch, u, s)
+            one = copy(
+                here, here, send_sem.at[kind], recv_sem.at[slot_of(epoch, me), kind], device(epoch, none, none)
             )
+            guarded(both(u[3], s[3]), one.wait_recv)
+
+    def forward(epoch):
+        for (a, _, kind), (_, s, _) in zip(images_in, images):
+            if s is none:
+                continue
+            source = centre.at[epoch, :, lanes_of(s)]
+            if a is not none:
+                source = vertical.at[a[2], epoch, :, lanes_of(s)]
+            one = copy(
+                source, landed(epoch, a, s), send_sem.at[kind], recv_sem.at[slot_of(epoch, me), kind],
+                device(me, none, s),
+            )
+            guarded(both(a[3], s[3]), one.start)
 
     def small(epoch, sender):
         return [
@@ -596,7 +602,7 @@
     def along_of(shift):
         return HALF - shift
 
-    behind = partners - 1 - ahead_of_me
+    behind = partners * across - 1 - ahead_of_me
 
     @pl.when(behind > 0)
     def _():
@@ -616,46 +622,44 @@
             send_early(epoch)
             coded(epoch, me).start()
 
-    for u, s, kind in images_in[1:]:
-        guarded(both(u[3], s[3]), lambda u=u, s=s, kind=kind: own_piece(u, s, kind, True).wait_recv())
-
-    tile = tile_of(me)
-    lay_own(0, jnp.clip(tile, 0, tile_dev - 1))
-    for at, model in models(0, toeplitz[me], down_of(offsets[0, me]), along_of(offsets[1, me])):
-        left = science[me, at] - model
-        residual[me, at] = left
-        share = weight[me, at]
-        for t in range(tile_dev):
-            here = (tile == t).astype(f32)
-            numer[t, at] = share * left * here
-            denom[t, at] = share * here
+    def own_board(tile):
+        return jnp.clip(tile, 0, tile_dev - 1)
 
     def partner(step):
         return jnp.where(me + step < n_epoch, me + step, n_epoch - 1 - step)
 
-    def process(step):
+    def wait_small(step):
         epoch = partner(step)
         for one in small(me, epoch) + [coefficient_tile(me, epoch)]:
             one.wait_recv()
+
+    def wait_image(step):
+        wait_pieces(partner(step), False)
+        forward(partner(step))
+
+    def wait_side(step):
+        wait_pieces(partner(step), True)
+
+    def theirs(step):
+        epoch = partner(step)
         last = exp_dev
         kernels[8 * last : 8 * last + 8] = mixed(
-            [
-                mix_of(coefs_in[epoch], lambda j: basis_index_in[epoch, me, j])
-            ]
+            [mix_of(coefs_in[epoch], lambda j: basis_index_in[epoch, me, j])]
         )
         spread(last, last)
-        tile = tile_of(epoch)
-        lay_own(0, jnp.clip(tile, 0, tile_dev - 1))
         for at, model in models(
-            0, toeplitz[last], down_of(offsets_in[epoch, 0, me]), along_of(offsets_in[epoch, 1, me])
+            own_board(tile_of(epoch)),
+            toeplitz[last],
+            down_of(offsets_in[epoch, 0, me]),
+            along_of(offsets_in[epoch, 1, me]),
         ):
             model_out[epoch, at] = model
 
-        wait_image(epoch)
-
-        lay_other(1, epoch)
+    def ours(step):
+        epoch = partner(step)
+        lay_other(tile_dev, epoch)
         for at, model in models(
-            1, toeplitz[epoch], down_of(offsets[0, epoch]), along_of(offsets[1, epoch])
+            tile_dev, toeplitz[epoch], down_of(offsets[0, epoch]), along_of(offsets[1, epoch])
         ):
             residual[epoch, at] = science[epoch, at] - model
 
@@ -670,13 +674,52 @@
             numer[t] = numer[t] + value * here
             denom[t] = denom[t] + share * here
 
+    def first():
+        tile = tile_of(me)
+        for at, model in models(own_board(tile), toeplitz[me], down_of(offsets[0, me]), along_of(offsets[1, me])):
+            left = science[me, at] - model
+            residual[me, at] = left
+            share = weight[me, at]
+            for t in range(tile_dev):
+                here = (tile == t).astype(f32)
+                numer[t, at] = share * left * here
+                denom[t, at] = share * here
+
+    for u, s, kind in images_in[1:]:
+        guarded(both(u[3], s[3]), lambda u=u, s=s, kind=kind: own_piece(u, s, kind, True).wait_recv())
+
     if n_epoch <= 4:
+        if n_epoch > 1:
+            wait_small(1)
+        for t in range(tile_dev):
+            lay_own(t, t)
+        if n_epoch > 1:
+            theirs(1)
+        first()
         for step in range(1, n_epoch):
-            process(step)
+            wait_image(step)
+            if step + 1 < n_epoch:
+                wait_small(step + 1)
+            wait_side(step)
+            ours(step)
+            if step + 1 < n_epoch:
+                theirs(step + 1)
         for step in range(1, n_epoch):
             gather(step)
     else:
-        lax.fori_loop(1, n_epoch, lambda step, carry: (process(step), carry)[1], 0)
+        for t in range(tile_dev):
+            lay_own(t, t)
+        first()
+
+        def body(step, carry):
+            wait_small(step)
+            theirs(step)
+            wait_image(step)
+            wait_side(step)
+            ours(step)
+            return carry
+
+        lax.fori_loop(1, n_epoch, body, 0)
         lax.fori_loop(1, n_epoch, lambda step, carry: (gather(step), carry)[1], 0)
 
     for t in range(tile_dev):
@@ -690,13 +733,13 @@
 
             def gone(u=u, s=s, kind=kind):
                 if u is none and s is none:
-                    source = chosen.at[rest]
+                    source = centre.at[rest]
                 elif s is none:
-                    source = chosen_edge.at[u[1], rest]
+                    source = vertical.at[0, rest]
                 elif u is none:
-                    source = chosen.at[rest, :, lanes_of(s)]
+                    source = lateral.at[0, rest]
                 else:
-                    source = chosen_edge.at[u[1], rest, :, lanes_of(s)]
+                    source = corner.at[0, 0, rest]
                 copy(source, source, send_sem.at[kind], recv_sem.at[0, kind], device(me, u, s)).wait_send()
 
             guarded(both(u[3], s[3]), gone)
@@ -780,7 +823,7 @@
             pltpu.VMEM((exp_dev, 8, LANES), f32),
             pltpu.VMEM((n_pairs * SLOT, LANES), bf16),
             pltpu.VMEM((8 * exp_dev + 8, n_pairs * SLOT), f32),
-            pltpu.VMEM((2, width // LANES + 1, 2 * rim + height + 8, LANES), f32),
+            pltpu.VMEM((tile_dev + 1, width // LANES + 1, 2 * rim + height + 8, LANES), f32),
             pltpu.VMEM((exp_dev + 1, n_poly * 8, n_pairs * SLOT), bf16),
             pltpu.VMEM((exp_dev, height, width), f32),
             pltpu.VMEM((n_epoch, height, width), jnp.int32),

time: 14.6 us -> 15.5 us (1.062)
  the two profiles are of different devices: /device:TPU:25 before, /device:TPU:9 now
where the time goes in v4:
time: 15.5 us; the launch traced here: 15.3 us
  Pallas kernels  14.7 us (95%)
  between operations  0.64 us (4%)
    pallas_call x1, Pallas kernels, local(): pl.pallas_call(functools.partial(kernel, sizes), out_shape=(pltpu.VMEM(sc...  14 us
    pallas_call x1, Pallas kernels, local(): pl.pallas_call(leave, out_shape=(jax.ShapeDtypeStruct(science.shape, f32)...  0.7 us

profile of v4, /device:TPU:9, one launch (start us, length us, event | category | flops | bytes accessed | tf_op | source)
XLA Modules:
  0.0 15.3 jit_solution(17535723761044122610)
XLA Ops:
  0.6 14.0 %shard_map.104 = (f32[4,24,256]{2,1,0:T(8,128)S(1)}, f32[2,24,256]{2,1,0:T(8,128)S(1)}) custom-call(s32[16]{0:T(128)} %intersection_hbm.1, s32[2,4]{1,0:T(2,128)} %bitcast.5, s32[4,16]{1,0:T(4,128)} %basis_index_hbm.1, f32[6,4,16]{2,1,0:T(4,128)} %bitcast.4, bf16[2,24,256]{2,1,0:T(8,128)(2,1)} %template_hbm.1, f32[4,24,256]{2,1,0:T(8,128)} %science_hbm.1, ...), custom_call_target="tpu_custom_call" | custom-call | tf_op jit(solution)/shard_map/pallas_call | solution.py:792
  14.6 0.7 %shard_map.105 = (f32[4,24,256]{2,1,0:T(8,128)}, f32[2,24,256]{2,1,0:T(8,128)}) custom-call(f32[4,24,256]{2,1,0:T(8,128)S(1)} %get-tuple-element.4.residual, f32[2,24,256]{2,1,0:T(8,128)S(1)} %get-tuple-element.5.coadd), custom_call_target="tpu_custom_call" | custom-call | tf_op jit(solution)/shard_map/pallas_call | solution.py:848

commit v5 on v3

--- a/solution.py
+++ b/solution.py
@@ -105,6 +105,7 @@
     code,
     code_in,
     model_out,
+    model_in,
     numer,
     denom,
     local_sem,
@@ -199,7 +200,7 @@
             lambda u=u, s=s: signal(token.at[me], me, u, s),
         )
     for epoch in range(n_epoch - 1):
-        pl.when(epoch < me)(lambda epoch=epoch: to_epoch(token.at[me], epoch))
+        pl.when(epoch < me)(lambda epoch=epoch: signal(token.at[me], epoch, none, none))
 
     def slot_of(sender, receiver):
         return sender - (sender > receiver).astype(jnp.int32)
@@ -227,7 +228,7 @@
         j = 0 if s is none else 1 + sides.index(s)
         images.append((u, s, i * (1 + n_side) + j))
     n_image = (1 + n_up) * (1 + n_side)
-    CODE, COEF, OFFS, INDX = n_image, n_image + 1, n_image + 2, n_image + 3
+    CODE, COEF, OFFS, INDX, MODEL = (n_image + i for i in range(5))
 
     def image(epoch, u, s, kind, sender, at=None):
         source_at = epoch if at is None else at
@@ -301,6 +302,12 @@
             device(epoch, none, none),
         )
 
+    def returned(epoch, sender):
+        return copy(
+            model_out.at[epoch], model_in.at[sender], send_sem.at[MODEL], recv_sem.at[slot_of(sender, epoch), MODEL],
+            device(epoch, none, none),
+        )
+
     def own_piece(u, s, kind, incoming):
         if s is none:
             source, dest = own_edge.at[0 if incoming else u[1]], own_vertical.at[u[2]]
@@ -342,12 +349,9 @@
         for p in range(n_poly):
             coefs[exposure, p : p + 1, 0:n_sel] = coefficients[p, exposure : exposure + 1, :]
 
-    def send_early(epoch):
-        coefficient_tile(epoch, me).start()
-        send_image(epoch)
-
     for epoch in range(n_epoch - 1):
-        pl.when(epoch < me)(lambda epoch=epoch: send_early(epoch))
+        pl.when(epoch < me)(lambda epoch=epoch: coefficient_tile(epoch, me).start())
+    pl.when(me > 0)(lambda: send_image(0))
     loads[2].wait()
     loads[3].wait()
     loads[4].wait()
@@ -356,7 +360,12 @@
         weight[epoch] = share
         code[epoch] = encode(science[epoch], share)
     for epoch in range(n_epoch - 1):
-        pl.when(epoch < me)(lambda epoch=epoch: coded(epoch, me).start())
+
+        @pl.when(epoch < me)
+        def _(epoch=epoch):
+            if epoch > 0:
+                send_image(epoch)
+            coded(epoch, me).start()
 
     for t in range(tile_dev):
         wide = template[t].astype(f32)
@@ -611,17 +620,22 @@
 
         @pl.when(me + step < n_epoch)
         def _(epoch=me + step):
-            pl.semaphore_wait(token.at[epoch], partners)
+            pl.semaphore_wait(token.at[epoch], 1)
             send_small(epoch)
-            send_early(epoch)
+            coefficient_tile(epoch, me).start()
             coded(epoch, me).start()
 
     for u, s, kind in images_in[1:]:
         guarded(both(u[3], s[3]), lambda u=u, s=s, kind=kind: own_piece(u, s, kind, True).wait_recv())
 
+    for t in range(tile_dev):
+        lay_own(t, t)
+
+    def own_board(tile):
+        return jnp.clip(tile, 0, tile_dev - 1)
+
     tile = tile_of(me)
-    lay_own(0, jnp.clip(tile, 0, tile_dev - 1))
-    for at, model in models(0, toeplitz[me], down_of(offsets[0, me]), along_of(offsets[1, me])):
+    for at, model in models(own_board(tile), toeplitz[me], down_of(offsets[0, me]), along_of(offsets[1, me])):
         left = science[me, at] - model
         residual[me, at] = left
         share = weight[me, at]
@@ -633,31 +647,44 @@
     def partner(step):
         return jnp.where(me + step < n_epoch, me + step, n_epoch - 1 - step)
 
-    def process(step):
+    def theirs(step):
         epoch = partner(step)
         for one in small(me, epoch) + [coefficient_tile(me, epoch)]:
             one.wait_recv()
         last = exp_dev
         kernels[8 * last : 8 * last + 8] = mixed(
-            [
-                mix_of(coefs_in[epoch], lambda j: basis_index_in[epoch, me, j])
-            ]
+            [mix_of(coefs_in[epoch], lambda j: basis_index_in[epoch, me, j])]
         )
         spread(last, last)
-        tile = tile_of(epoch)
-        lay_own(0, jnp.clip(tile, 0, tile_dev - 1))
         for at, model in models(
-            0, toeplitz[last], down_of(offsets_in[epoch, 0, me]), along_of(offsets_in[epoch, 1, me])
+            own_board(tile_of(epoch)),
+            toeplitz[last],
+            down_of(offsets_in[epoch, 0, me]),
+            along_of(offsets_in[epoch, 1, me]),
         ):
             model_out[epoch, at] = model
-
+        pl.when(epoch > me)(lambda: returned(epoch, me).start())
+
+    def ours(step):
+        epoch = partner(step)
         wait_image(epoch)
-
-        lay_other(1, epoch)
+        lay_other(tile_dev, epoch)
         for at, model in models(
-            1, toeplitz[epoch], down_of(offsets[0, epoch]), along_of(offsets[1, epoch])
+            tile_dev, toeplitz[epoch], down_of(offsets[0, epoch]), along_of(offsets[1, epoch])
         ):
             residual[epoch, at] = science[epoch, at] - model
+
+    def settle(step):
+        epoch = partner(step)
+        returned(me, epoch).wait_recv()
+        residual[epoch] = science[epoch] - model_in[epoch]
+
+    def mine(step):
+        pl.when(partner(step) > me)(lambda: ours(step))
+
+    def finish(step):
+        gather(step)
+        pl.when(partner(step) < me)(lambda: settle(step))
 
     def gather(step):
         epoch = partner(step)
@@ -672,12 +699,15 @@
 
     if n_epoch <= 4:
         for step in range(1, n_epoch):
-            process(step)
+            theirs(step)
         for step in range(1, n_epoch):
-            gather(step)
+            mine(step)
+        for step in range(1, n_epoch):
+            finish(step)
     else:
-        lax.fori_loop(1, n_epoch, lambda step, carry: (process(step), carry)[1], 0)
-        lax.fori_loop(1, n_epoch, lambda step, carry: (gather(step), carry)[1], 0)
+        lax.fori_loop(1, n_epoch, lambda step, carry: (theirs(step), carry)[1], 0)
+        lax.fori_loop(1, n_epoch, lambda step, carry: (mine(step), carry)[1], 0)
+        lax.fori_loop(1, n_epoch, lambda step, carry: (finish(step), carry)[1], 0)
 
     for t in range(tile_dev):
         coadd[t] = numer[t] / (denom[t] + 1.0)
@@ -686,30 +716,40 @@
         guarded(both(u[3], s[3]), lambda u=u, s=s, kind=kind: own_piece(u, s, kind, False).wait_send())
     if n_epoch > 1:
         rest = pl.ds(0, n_epoch - 1)
-        for u, s, kind in images:
-
-            def gone(u=u, s=s, kind=kind):
-                if u is none and s is none:
-                    source = chosen.at[rest]
-                elif s is none:
-                    source = chosen_edge.at[u[1], rest]
-                elif u is none:
-                    source = chosen.at[rest, :, lanes_of(s)]
-                else:
-                    source = chosen_edge.at[u[1], rest, :, lanes_of(s)]
-                copy(source, source, send_sem.at[kind], recv_sem.at[0, kind], device(me, u, s)).wait_send()
-
-            guarded(both(u[3], s[3]), gone)
+
+        def drain(source, kind, u, s):
+            copy(source, source, send_sem.at[kind], recv_sem.at[0, kind], device(me, u, s)).wait_send()
+
+        for number in range(1, n_epoch):
+
+            @pl.when(me == number)
+            def _(number=number):
+                lead = pl.ds(0, number)
+                for u, s, kind in images:
+                    if u is none and s is none:
+                        source = chosen.at[lead]
+                    elif s is none:
+                        source = chosen_edge.at[u[1], lead]
+                    elif u is none:
+                        source = chosen.at[lead, :, lanes_of(s)]
+                    else:
+                        source = chosen_edge.at[u[1], lead, :, lanes_of(s)]
+                    guarded(
+                        both(u[3], s[3]),
+                        lambda u=u, s=s, kind=kind, source=source: drain(source, kind, u, s),
+                    )
+
+            @pl.when(me == n_epoch - 1 - number)
+            def _(number=number):
+                drain(model_out.at[pl.ds(0, number)], MODEL, none, none)
+
         for held, kind in (
             (offsets_in, OFFS),
             (basis_index_in, INDX),
             (coefs, COEF),
             (code, CODE),
         ):
-            source = held.at[rest]
-            copy(
-                source, source, send_sem.at[kind], recv_sem.at[0, kind], device(me, none, none)
-            ).wait_send()
+            drain(held.at[rest], kind, none, none)
 
 
 def leave(residual, coadd, residual_out, coadd_out, sem):
@@ -780,17 +820,18 @@
             pltpu.VMEM((exp_dev, 8, LANES), f32),
             pltpu.VMEM((n_pairs * SLOT, LANES), bf16),
             pltpu.VMEM((8 * exp_dev + 8, n_pairs * SLOT), f32),
-            pltpu.VMEM((2, width // LANES + 1, 2 * rim + height + 8, LANES), f32),
+            pltpu.VMEM((tile_dev + 1, width // LANES + 1, 2 * rim + height + 8, LANES), f32),
             pltpu.VMEM((exp_dev + 1, n_poly * 8, n_pairs * SLOT), bf16),
             pltpu.VMEM((exp_dev, height, width), f32),
             pltpu.VMEM((n_epoch, height, width), jnp.int32),
             pltpu.VMEM((n_epoch, height, width), jnp.int32),
             pltpu.VMEM((n_epoch, height, width), f32),
+            pltpu.VMEM((n_epoch, height, width), f32),
             pltpu.VMEM(template.shape, f32),
             pltpu.VMEM(template.shape, f32),
             dma((9,)),
-            dma((n_image + 4,)),
-            dma((max(n_epoch - 1, 1), n_image + 4)),
+            dma((n_image + 5,)),
+            dma((max(n_epoch - 1, 1), n_image + 5)),
             dma((n_image,)),
             dma((n_image,)),
             pltpu.SemaphoreType.REGULAR((n_epoch,)),

time: 14.6 us -> 13.8 us (0.945)
  the two profiles are of different devices: /device:TPU:25 before, /device:TPU:0 now
where the time goes in v5:
time: 13.8 us; the launch traced here: 13.6 us
  Pallas kernels  13 us (94%)
  between operations  0.64 us (5%)
    pallas_call x1, Pallas kernels, local(): pl.pallas_call(functools.partial(kernel, sizes), out_shape=(pltpu.VMEM(sc...  12.3 us
    pallas_call x1, Pallas kernels, local(): pl.pallas_call(leave, out_shape=(jax.ShapeDtypeStruct(science.shape, f32)...  0.7 us

profile of v5, /device:TPU:0, one launch (start us, length us, event | category | flops | bytes accessed | tf_op | source)
XLA Modules:
  0.0 13.6 jit_solution(11119875547562572034)
XLA Ops:
  0.6 12.3 %shard_map.104 = (f32[4,24,256]{2,1,0:T(8,128)S(1)}, f32[2,24,256]{2,1,0:T(8,128)S(1)}) custom-call(s32[16]{0:T(128)} %intersection_hbm.1, s32[2,4]{1,0:T(2,128)} %bitcast.5, s32[4,16]{1,0:T(4,128)} %basis_index_hbm.1, f32[6,4,16]{2,1,0:T(4,128)} %bitcast.4, bf16[2,24,256]{2,1,0:T(8,128)(2,1)} %template_hbm.1, f32[4,24,256]{2,1,0:T(8,128)} %science_hbm.1, ...), custom_call_target="tpu_custom_call" | custom-call | tf_op jit(solution)/shard_map/pallas_call | solution.py:789
  12.9 0.7 %shard_map.105 = (f32[4,24,256]{2,1,0:T(8,128)}, f32[2,24,256]{2,1,0:T(8,128)}) custom-call(f32[4,24,256]{2,1,0:T(8,128)S(1)} %get-tuple-element.4.residual, f32[2,24,256]{2,1,0:T(8,128)S(1)} %get-tuple-element.5.coadd), custom_call_target="tpu_custom_call" | custom-call | tf_op jit(solution)/shard_map/pallas_call | solution.py:846

commit v6 on v5

--- a/solution.py
+++ b/solution.py
@@ -13,6 +13,7 @@
 LANES = 128
 SLOT = 64
 GROUPS = 4
+SIDE = 16
 SCIENCE_TOP = 6.0
 WEIGHT_TOP = 0.5
 LEVELS = 65535.0
@@ -88,7 +89,11 @@
     basis,
     chosen,
     chosen_edge,
+    chosen_side,
+    chosen_corner,
     own_edge,
+    own_side,
+    own_diagonal,
     centre,
     vertical,
     lateral,
@@ -97,6 +102,7 @@
     own_lateral,
     own_corner,
     coefs,
+    coef_row,
     table,
     kernels,
     slab,
@@ -205,11 +211,27 @@
     def slot_of(sender, receiver):
         return sender - (sender > receiver).astype(jnp.int32)
 
-    def lanes_of(s):
+    lane = lax.broadcasted_iota(jnp.int32, (8, LANES), 1)
+    sub = lax.broadcasted_iota(jnp.int32, (8, LANES), 0)
+
+    def within(base):
+        return jnp.bitwise_and(lane - base, LANES - 1) < SIDE
+
+    def side_tile(wide, which):
+        first, last = wide[:, :LANES], wide[:, width - LANES :]
         if n_band == 2:
-            start = (1 - band) * (width - LANES)
-            return pl.ds(pl.multiple_of(start, LANES), LANES)
-        return slice(0, LANES) if s[1] == 0 else slice(width - LANES, width)
+            return jnp.where(band == 0, last, first), (1 - band) * (LANES - SIDE)
+        return (first, 0) if which == 0 else (last, LANES - SIDE)
+
+    def packed(wide, which):
+        tile, base = side_tile(wide, which)
+        out = jnp.zeros((8, LANES), f32)
+        for i in range(wide.shape[0] // 8):
+            part = tile[8 * i : 8 * i + 8]
+            if i > 0:
+                part = pltpu.roll(part, SIDE * i, 1)
+            out = jnp.where(within(base + SIDE * i), part, out)
+        return out.astype(bf16)
 
     def copy(source, dest, sent, received, to):
         return pltpu.make_async_remote_copy(
@@ -237,9 +259,9 @@
         elif s is none:
             source, dest = chosen_edge.at[u[1], source_at], vertical.at[u[2], sender]
         elif u is none:
-            source, dest = chosen.at[source_at, :, lanes_of(s)], lateral.at[s[2], sender]
+            source, dest = chosen_side.at[s[1], source_at], lateral.at[s[2], sender]
         else:
-            source = chosen_edge.at[u[1], source_at, :, lanes_of(s)]
+            source = chosen_corner.at[u[1], s[1], source_at]
             dest = corner.at[u[2], s[2], sender]
         return copy(
             source, dest, send_sem.at[kind], recv_sem.at[slot_of(sender, epoch), kind], device(epoch, u, s)
@@ -292,7 +314,7 @@
 
     def coefficient_tile(epoch, sender):
         return copy(
-            coefs.at[epoch], coefs_in.at[sender], send_sem.at[COEF], recv_sem.at[slot_of(sender, epoch), COEF],
+            coef_row.at[epoch], coefs_in.at[sender], send_sem.at[COEF], recv_sem.at[slot_of(sender, epoch), COEF],
             device(epoch, none, none),
         )
 
@@ -312,9 +334,9 @@
         if s is none:
             source, dest = own_edge.at[0 if incoming else u[1]], own_vertical.at[u[2]]
         elif u is none:
-            source, dest = template.at[:, :, lanes_of(s)], own_lateral.at[s[2]]
+            source, dest = own_side.at[0 if incoming else s[1]], own_lateral.at[s[2]]
         else:
-            source = own_edge.at[0 if incoming else u[1], :, :, lanes_of(s)]
+            source = own_diagonal.at[0 if incoming else u[1], 0 if incoming else s[1]]
             dest = own_corner.at[u[2], s[2]]
         if incoming:
             source = dest
@@ -341,13 +363,21 @@
         picked = template[jnp.clip(tile, 0, tile_dev - 1)]
         chosen[epoch] = picked
         wide = picked.astype(f32)
+        for side in range(n_side):
+            chosen_side[side, epoch] = packed(wide, side)
         for which in range(n_up):
-            chosen_edge[which, epoch] = rim(wide, which).astype(bf16)
+            edge = rim(wide, which)
+            chosen_edge[which, epoch] = edge.astype(bf16)
+            for side in range(n_side):
+                chosen_corner[which, side, epoch] = packed(edge, side)
     loads[5].wait()
     for exposure in range(exp_dev):
         coefs[exposure] = jnp.zeros((8, LANES), f32)
         for p in range(n_poly):
             coefs[exposure, p : p + 1, 0:n_sel] = coefficients[p, exposure : exposure + 1, :]
+        coef_row[exposure] = jnp.sum(
+            pltpu.roll(coefs[exposure], 0, 1, stride=n_sel, stride_axis=0), axis=0, keepdims=True
+        )
 
     for epoch in range(n_epoch - 1):
         pl.when(epoch < me)(lambda epoch=epoch: coefficient_tile(epoch, me).start())
@@ -369,8 +399,13 @@
 
     for t in range(tile_dev):
         wide = template[t].astype(f32)
+        for side in range(n_side):
+            own_side[side, t] = packed(wide, side)
         for which in range(n_up):
-            own_edge[which, t] = rim(wide, which).astype(bf16)
+            edge = rim(wide, which)
+            own_edge[which, t] = edge.astype(bf16)
+            for side in range(n_side):
+                own_diagonal[which, side, t] = packed(edge, side)
     for u, s, kind in images[1:]:
         guarded(
             both(both(u[3], s[3]), lower(u, s)),
@@ -436,8 +471,6 @@
         (slab.shape[0], slab.shape[1], 8, LANES), f32
     )
 
-    lane = lax.broadcasted_iota(jnp.int32, (8, LANES), 1)
-    sub = lax.broadcasted_iota(jnp.int32, (8, LANES), 0)
     n_pairs = (ks + 1) // 2
     n_tiles = n_pairs * SLOT // LANES
     later = jnp.bitwise_and(lane, 7) >= sub
@@ -456,6 +489,13 @@
         mix = mix + pltpu.roll(mix, half, 1)
         high = mix.astype(bf16).astype(f32)
         return high, mix - high
+
+    def unpacked(line):
+        wide = jnp.broadcast_to(line, (8, LANES))
+        out = wide
+        for p in range(1, n_poly):
+            out = jnp.where(sub == p, pltpu.roll(wide, LANES - n_sel * p, 1), out)
+        return out
 
     def mixed(pairs):
         rows = jnp.concatenate([p[0] for p in pairs] + [p[1] for p in pairs], axis=0)
@@ -528,20 +568,26 @@
     span = height + 8 * GROUPS - 8
     at_lane = lax.broadcasted_iota(jnp.int32, (span, LANES), 1)
 
+    beside = [(0, LANES - SIDE), (1, 0)]
+    if n_band == 2:
+        beside = [(1 - band, band * (LANES - SIDE))]
+
     def lay(board, middle, up, side, edge, at):
         for rows, body, rims in (
-            (0, up(0), (edge(0, 1), edge(0, 0))),
-            (EDGE_ROWS, middle, (side(1), side(0))),
-            (EDGE_ROWS + height, up(1), (edge(1, 1), edge(1, 0))),
+            (0, up(0), [(edge(0, k).astype(f32), base) for k, base in beside]),
+            (EDGE_ROWS, middle, [(side(k).astype(f32), base) for k, base in beside]),
+            (EDGE_ROWS + height, up(1), [(edge(1, k).astype(f32), base) for k, base in beside]),
         ):
             wide = body.astype(f32)
             size = wide.shape[0]
             for t in range(n_lane):
                 slab[board, t, rows : rows + size, :] = wide[:, t * LANES : (t + 1) * LANES]
-            first = lax.broadcasted_iota(jnp.int32, (size, LANES), 1) < half
-            slab[board, n_lane, rows : rows + size, :] = jnp.where(
-                first, rims[0].astype(f32), rims[1].astype(f32)
-            )
+            for i in range(size // 8):
+                part = jnp.zeros((8, LANES), f32)
+                for held, base in rims:
+                    turned = held if i == 0 else pltpu.roll(held, LANES - SIDE * i, 1)
+                    part = jnp.where(within(base), turned, part)
+                slab[board, n_lane, rows + 8 * i : rows + 8 * i + 8, :] = part
 
     def lay_own(board, tile):
         lay(
@@ -653,7 +699,7 @@
             one.wait_recv()
         last = exp_dev
         kernels[8 * last : 8 * last + 8] = mixed(
-            [mix_of(coefs_in[epoch], lambda j: basis_index_in[epoch, me, j])]
+            [mix_of(unpacked(coefs_in[epoch]), lambda j: basis_index_in[epoch, me, j])]
         )
         spread(last, last)
         for at, model in models(
@@ -700,8 +746,12 @@
     if n_epoch <= 4:
         for step in range(1, n_epoch):
             theirs(step)
-        for step in range(1, n_epoch):
+        if n_epoch > 1:
+            pl.when(me == 0)(lambda: mine(1))
+        for step in range(n_epoch - 1, 1, -1):
             mine(step)
+        if n_epoch > 1:
+            pl.when(me > 0)(lambda: mine(1))
         for step in range(1, n_epoch):
             finish(step)
     else:
@@ -731,9 +781,9 @@
                     elif s is none:
                         source = chosen_edge.at[u[1], lead]
                     elif u is none:
-                        source = chosen.at[lead, :, lanes_of(s)]
+                        source = chosen_side.at[s[1], lead]
                     else:
-                        source = chosen_edge.at[u[1], lead, :, lanes_of(s)]
+                        source = chosen_corner.at[u[1], s[1], lead]
                     guarded(
                         both(u[3], s[3]),
                         lambda u=u, s=s, kind=kind, source=source: drain(source, kind, u, s),
@@ -746,7 +796,7 @@
         for held, kind in (
             (offsets_in, OFFS),
             (basis_index_in, INDX),
-            (coefs, COEF),
+            (coef_row, COEF),
             (code, CODE),
         ):
             drain(held.at[rest], kind, none, none)
@@ -784,7 +834,7 @@
     basis = basis.transpose(1, 2, 0)
     n_up, n_side = min(n_strip - 1, 2), min(n_band - 1, 2)
     n_image = (1 + n_up) * (1 + n_side)
-    edges = max(n_up, 1)
+    edges, sides = max(n_up, 1), max(n_side, 1)
     rim = EDGE_ROWS
     residual, coadd = pl.pallas_call(
         functools.partial(kernel, sizes),
@@ -801,7 +851,7 @@
             pltpu.SMEM(basis_index.shape, jnp.int32),
             pltpu.SMEM((n_epoch,) + basis_index.shape, jnp.int32),
             pltpu.VMEM(coefficients.shape, f32),
-            pltpu.VMEM((n_epoch, 8, LANES), f32),
+            pltpu.VMEM((n_epoch, 1, LANES), f32),
             pltpu.VMEM(template.shape, bf16),
             pltpu.VMEM(science.shape, f32),
             pltpu.VMEM(science.shape, f32),
@@ -809,15 +859,20 @@
             pltpu.VMEM(basis.shape, f32),
             pltpu.VMEM((n_epoch, height, width), bf16),
             pltpu.VMEM((edges, n_epoch, rim, width), bf16),
+            pltpu.VMEM((sides, n_epoch, 8, LANES), bf16),
+            pltpu.VMEM((edges, sides, n_epoch, 8, LANES), bf16),
             pltpu.VMEM((edges, tile_dev, rim, width), bf16),
+            pltpu.VMEM((sides, tile_dev, 8, LANES), bf16),
+            pltpu.VMEM((edges, sides, tile_dev, 8, LANES), bf16),
             pltpu.VMEM((n_epoch, height, width), bf16),
             pltpu.VMEM((2, n_epoch, rim, width), bf16),
-            pltpu.VMEM((2, n_epoch, height, LANES), bf16),
-            pltpu.VMEM((2, 2, n_epoch, rim, LANES), bf16),
+            pltpu.VMEM((2, n_epoch, 8, LANES), bf16),
+            pltpu.VMEM((2, 2, n_epoch, 8, LANES), bf16),
             pltpu.VMEM((2, tile_dev, rim, width), bf16),
-            pltpu.VMEM((2, tile_dev, height, LANES), bf16),
-            pltpu.VMEM((2, 2, tile_dev, rim, LANES), bf16),
+            pltpu.VMEM((2, tile_dev, 8, LANES), bf16),
+            pltpu.VMEM((2, 2, tile_dev, 8, LANES), bf16),
             pltpu.VMEM((exp_dev, 8, LANES), f32),
+            pltpu.VMEM((exp_dev, 1, LANES), f32),
             pltpu.VMEM((n_pairs * SLOT, LANES), bf16),
             pltpu.VMEM((8 * exp_dev + 8, n_pairs * SLOT), f32),
             pltpu.VMEM((tile_dev + 1, width // LANES + 1, 2 * rim + height + 8, LANES), f32),

time: 13.8 us -> 13.3 us (0.964)
  Pallas kernels: 13 us -> 12.5 us
    pallas_call x1, Pallas kernels: 12.3 us -> 11.8 us  [local(): pl.pallas_call(functools.partial(kernel, sizes), out_shape=(pltpu.VMEM(sc...]
where the time goes in v6:
time: 13.3 us; the launch traced here: 13.1 us
  Pallas kernels  12.5 us (94%)
  between operations  0.64 us (5%)
    pallas_call x1, Pallas kernels, local(): pl.pallas_call(functools.partial(kernel, sizes), out_shape=(pltpu.VMEM(sc...  11.8 us
    pallas_call x1, Pallas kernels, local(): pl.pallas_call(leave, out_shape=(jax.ShapeDtypeStruct(science.shape, f32)...  0.7 us

profile of v6, /device:TPU:0, one launch (start us, length us, event | category | flops | bytes accessed | tf_op | source)
XLA Modules:
  0.0 13.1 jit_solution(1792778724971134774)
XLA Ops:
  0.6 11.8 %shard_map.104 = (f32[4,24,256]{2,1,0:T(8,128)S(1)}, f32[2,24,256]{2,1,0:T(8,128)S(1)}) custom-call(s32[16]{0:T(128)} %intersection_hbm.1, s32[2,4]{1,0:T(2,128)} %bitcast.5, s32[4,16]{1,0:T(4,128)} %basis_index_hbm.1, f32[6,4,16]{2,1,0:T(4,128)} %bitcast.4, bf16[2,24,256]{2,1,0:T(8,128)(2,1)} %template_hbm.1, f32[4,24,256]{2,1,0:T(8,128)} %science_hbm.1, ...), custom_call_target="tpu_custom_call" | custom-call | tf_op jit(solution)/shard_map/pallas_call | solution.py:839
  12.4 0.7 %shard_map.105 = (f32[4,24,256]{2,1,0:T(8,128)}, f32[2,24,256]{2,1,0:T(8,128)}) custom-call(f32[4,24,256]{2,1,0:T(8,128)S(1)} %get-tuple-element.4.residual, f32[2,24,256]{2,1,0:T(8,128)S(1)} %get-tuple-element.5.coadd), custom_call_target="tpu_custom_call" | custom-call | tf_op jit(solution)/shard_map/pallas_call | solution.py:901

commit v7 on v6

--- a/solution.py
+++ b/solution.py
@@ -662,8 +662,7 @@
             both(both(u[3], s[3]), jnp.logical_not(lower(u, s))),
             lambda u=u, s=s, kind=kind: own_piece(u, s, kind, False).start(),
         )
-    for step in range(1, n_epoch):
-
+    def offer(step):
         @pl.when(me + step < n_epoch)
         def _(epoch=me + step):
             pl.semaphore_wait(token.at[epoch], 1)
@@ -671,32 +670,36 @@
             coefficient_tile(epoch, me).start()
             coded(epoch, me).start()
 
+    early = n_epoch - 2 if n_epoch == 4 else n_epoch - 1
+    for step in range(1, early + 1):
+        offer(step)
+
     for u, s, kind in images_in[1:]:
         guarded(both(u[3], s[3]), lambda u=u, s=s, kind=kind: own_piece(u, s, kind, True).wait_recv())
 
-    for t in range(tile_dev):
-        lay_own(t, t)
-
     def own_board(tile):
         return jnp.clip(tile, 0, tile_dev - 1)
 
-    tile = tile_of(me)
-    for at, model in models(own_board(tile), toeplitz[me], down_of(offsets[0, me]), along_of(offsets[1, me])):
-        left = science[me, at] - model
-        residual[me, at] = left
-        share = weight[me, at]
+    def first():
+        tile = tile_of(me)
+        for at, model in models(own_board(tile), toeplitz[me], down_of(offsets[0, me]), along_of(offsets[1, me])):
+            left = science[me, at] - model
+            residual[me, at] = left
+            share = weight[me, at]
+            for t in range(tile_dev):
+                here = (tile == t).astype(f32)
+                numer[t, at] = share * left * here
+                denom[t, at] = share * here
+
+    def lay_tiles():
         for t in range(tile_dev):
-            here = (tile == t).astype(f32)
-            numer[t, at] = share * left * here
-            denom[t, at] = share * here
+            lay_own(t, t)
 
     def partner(step):
         return jnp.where(me + step < n_epoch, me + step, n_epoch - 1 - step)
 
     def theirs(step):
         epoch = partner(step)
-        for one in small(me, epoch) + [coefficient_tile(me, epoch)]:
-            one.wait_recv()
         last = exp_dev
         kernels[8 * last : 8 * last + 8] = mixed(
             [mix_of(unpacked(coefs_in[epoch]), lambda j: basis_index_in[epoch, me, j])]
@@ -709,14 +712,26 @@
             along_of(offsets_in[epoch, 1, me]),
         ):
             model_out[epoch, at] = model
-        pl.when(epoch > me)(lambda: returned(epoch, me).start())
+
+    def wait_small(step):
+        epoch = partner(step)
+        for one in small(me, epoch) + [coefficient_tile(me, epoch)]:
+            one.wait_recv()
+
+    def answer(step):
+        pl.when(partner(step) > me)(lambda: returned(partner(step), me).start())
+
+    def host(step):
+        wait_small(step)
+        theirs(step)
+        answer(step)
 
     def ours(step):
         epoch = partner(step)
-        wait_image(epoch)
-        lay_other(tile_dev, epoch)
+        board = tile_dev + step - 1 if isinstance(step, int) else tile_dev
+        lay_other(board, epoch)
         for at, model in models(
-            tile_dev, toeplitz[epoch], down_of(offsets[0, epoch]), along_of(offsets[1, epoch])
+            board, toeplitz[epoch], down_of(offsets[0, epoch]), along_of(offsets[1, epoch])
         ):
             residual[epoch, at] = science[epoch, at] - model
 
@@ -726,7 +741,10 @@
         residual[epoch] = science[epoch] - model_in[epoch]
 
     def mine(step):
-        pl.when(partner(step) > me)(lambda: ours(step))
+        @pl.when(partner(step) > me)
+        def _():
+            wait_image(partner(step))
+            ours(step)
 
     def finish(step):
         gather(step)
@@ -743,21 +761,48 @@
             numer[t] = numer[t] + value * here
             denom[t] = denom[t] + share * here
 
-    if n_epoch <= 4:
-        for step in range(1, n_epoch):
-            theirs(step)
-        if n_epoch > 1:
-            pl.when(me == 0)(lambda: mine(1))
-        for step in range(n_epoch - 1, 1, -1):
-            mine(step)
-        if n_epoch > 1:
-            pl.when(me > 0)(lambda: mine(1))
+    if n_epoch == 4:
+
+        @pl.when(me == 0)
+        def _():
+            wait_small(1)
+            lay_tiles()
+            theirs(1)
+            first()
+            answer(1)
+            offer(3)
+            wait_small(2)
+            wait_image(1)
+            theirs(2)
+            ours(1)
+            answer(2)
+            host(3)
+            wait_image(3)
+            ours(3)
+            wait_image(2)
+            ours(2)
+
+        @pl.when(me > 0)
+        def _():
+            lay_tiles()
+            first()
+            for step in range(1, n_epoch):
+                host(step)
+            for step in range(2, 0, -1):
+                mine(step)
+
         for step in range(1, n_epoch):
             finish(step)
     else:
-        lax.fori_loop(1, n_epoch, lambda step, carry: (theirs(step), carry)[1], 0)
-        lax.fori_loop(1, n_epoch, lambda step, carry: (mine(step), carry)[1], 0)
-        lax.fori_loop(1, n_epoch, lambda step, carry: (finish(step), carry)[1], 0)
+        lay_tiles()
+        first()
+
+        def walk(stage):
+            lax.fori_loop(1, n_epoch, lambda step, carry: (stage(step), carry)[1], 0)
+
+        walk(host)
+        walk(mine)
+        walk(finish)
 
     for t in range(tile_dev):
         coadd[t] = numer[t] / (denom[t] + 1.0)
@@ -875,7 +920,7 @@
             pltpu.VMEM((exp_dev, 1, LANES), f32),
             pltpu.VMEM((n_pairs * SLOT, LANES), bf16),
             pltpu.VMEM((8 * exp_dev + 8, n_pairs * SLOT), f32),
-            pltpu.VMEM((tile_dev + 1, width // LANES + 1, 2 * rim + height + 8, LANES), f32),
+            pltpu.VMEM((tile_dev + max(n_epoch - 1, 1), width // LANES + 1, 2 * rim + height + 8, LANES), f32),
             pltpu.VMEM((exp_dev + 1, n_poly * 8, n_pairs * SLOT), bf16),
             pltpu.VMEM((exp_dev, height, width), f32),
             pltpu.VMEM((n_epoch, height, width), jnp.int32),

time: 13.3 us -> 12.9 us (0.970)
  Pallas kernels: 12.5 us -> 12.1 us
    pallas_call x1, Pallas kernels: 11.8 us -> 11.4 us  [local(): pl.pallas_call(functools.partial(kernel, sizes), out_shape=(pltpu.VMEM(sc...]
where the time goes in v7:
time: 12.9 us; the launch traced here: 12.8 us
  Pallas kernels  12.1 us (94%)
  between operations  0.64 us (5%)
    pallas_call x1, Pallas kernels, local(): pl.pallas_call(functools.partial(kernel, sizes), out_shape=(pltpu.VMEM(sc...  11.4 us
    pallas_call x1, Pallas kernels, local(): pl.pallas_call(leave, out_shape=(jax.ShapeDtypeStruct(science.shape, f32)...  0.7 us

profile of v7, /device:TPU:0, one launch (start us, length us, event | category | flops | bytes accessed | tf_op | source)
XLA Modules:
  0.0 12.8 jit_solution(14736520031822298795)
XLA Ops:
  0.6 11.4 %shard_map.104 = (f32[4,24,256]{2,1,0:T(8,128)S(1)}, f32[2,24,256]{2,1,0:T(8,128)S(1)}) custom-call(s32[16]{0:T(128)} %intersection_hbm.1, s32[2,4]{1,0:T(2,128)} %bitcast.5, s32[4,16]{1,0:T(4,128)} %basis_index_hbm.1, f32[6,4,16]{2,1,0:T(4,128)} %bitcast.4, bf16[2,24,256]{2,1,0:T(8,128)(2,1)} %template_hbm.1, f32[4,24,256]{2,1,0:T(8,128)} %science_hbm.1, ...), custom_call_target="tpu_custom_call" | custom-call | tf_op jit(solution)/shard_map/pallas_call | solution.py:884
  12.1 0.7 %shard_map.105 = (f32[4,24,256]{2,1,0:T(8,128)}, f32[2,24,256]{2,1,0:T(8,128)}) custom-call(f32[4,24,256]{2,1,0:T(8,128)S(1)} %get-tuple-element.4.residual, f32[2,24,256]{2,1,0:T(8,128)S(1)} %get-tuple-element.5.coadd), custom_call_target="tpu_custom_call" | custom-call | tf_op jit(solution)/shard_map/pallas_call | solution.py:946

commit v8 on v7

--- a/solution.py
+++ b/solution.py
@@ -158,8 +158,8 @@
             )
         )
     ]
-    for load in loads:
-        load.start()
+    for i in (5, 6, 8, 0, 1, 2, 3, 4, 7):
+        loads[i].start()
 
     def count(size, place):
         if size < 3:
@@ -307,8 +307,8 @@
         return [
             copy(held, into.at[sender], send_sem.at[kind], recv_sem.at[slot_of(sender, epoch), kind], device(epoch, none, none))
             for held, into, kind in (
-                (offsets_hbm, offsets_in, OFFS),
-                (basis_index_hbm, basis_index_in, INDX),
+                (offsets, offsets_in, OFFS),
+                (basis_index, basis_index_in, INDX),
             )
         ]
 
@@ -326,7 +326,7 @@
 
     def returned(epoch, sender):
         return copy(
-            model_out.at[epoch], model_in.at[sender], send_sem.at[MODEL], recv_sem.at[slot_of(sender, epoch), MODEL],
+            model_out.at[epoch], model_in.at[sender], send_sem.at[MODEL], recv_sem.at[slot_of(sender, epoch), 0],
             device(epoch, none, none),
         )
 
@@ -346,9 +346,22 @@
         for one in small(epoch, me):
             one.start()
 
+    loads[6].wait()
+    loads[8].wait()
     for epoch in range(n_epoch - 1):
         pl.when(epoch < me)(lambda epoch=epoch: send_small(epoch))
 
+    loads[5].wait()
+    for exposure in range(exp_dev):
+        coefs[exposure] = jnp.zeros((8, LANES), f32)
+        for p in range(n_poly):
+            coefs[exposure, p : p + 1, 0:n_sel] = coefficients[p, exposure : exposure + 1, :]
+        coef_row[exposure] = jnp.sum(
+            pltpu.roll(coefs[exposure], 0, 1, stride=n_sel, stride_axis=0), axis=0, keepdims=True
+        )
+
+    for epoch in range(n_epoch - 1):
+        pl.when(epoch < me)(lambda epoch=epoch: coefficient_tile(epoch, me).start())
     loads[0].wait()
     loads[1].wait()
 
@@ -370,17 +383,6 @@
             chosen_edge[which, epoch] = edge.astype(bf16)
             for side in range(n_side):
                 chosen_corner[which, side, epoch] = packed(edge, side)
-    loads[5].wait()
-    for exposure in range(exp_dev):
-        coefs[exposure] = jnp.zeros((8, LANES), f32)
-        for p in range(n_poly):
-            coefs[exposure, p : p + 1, 0:n_sel] = coefficients[p, exposure : exposure + 1, :]
-        coef_row[exposure] = jnp.sum(
-            pltpu.roll(coefs[exposure], 0, 1, stride=n_sel, stride_axis=0), axis=0, keepdims=True
-        )
-
-    for epoch in range(n_epoch - 1):
-        pl.when(epoch < me)(lambda epoch=epoch: coefficient_tile(epoch, me).start())
     pl.when(me > 0)(lambda: send_image(0))
     loads[2].wait()
     loads[3].wait()
@@ -389,13 +391,7 @@
         share = bad_mask[epoch].astype(f32) / variance[epoch]
         weight[epoch] = share
         code[epoch] = encode(science[epoch], share)
-    for epoch in range(n_epoch - 1):
-
-        @pl.when(epoch < me)
-        def _(epoch=epoch):
-            if epoch > 0:
-                send_image(epoch)
-            coded(epoch, me).start()
+    pl.when(me > 0)(lambda: coded(0, me).start())
 
     for t in range(tile_dev):
         wide = template[t].astype(f32)
@@ -521,7 +517,6 @@
                     jnp.concatenate(halves, axis=0).astype(bf16)
                 )
 
-    loads[6].wait()
     pairs = [
         mix_of(
             coefs[exposure],
@@ -554,7 +549,6 @@
         axis=0,
     ).astype(bf16)
     kernels[0 : 8 * exp_dev] = mixed(pairs)
-    loads[8].wait()
     for exposure in range(exp_dev):
         spread(exposure, exposure)
 
@@ -662,6 +656,13 @@
             both(both(u[3], s[3]), jnp.logical_not(lower(u, s))),
             lambda u=u, s=s, kind=kind: own_piece(u, s, kind, False).start(),
         )
+    for epoch in range(1, n_epoch - 1):
+
+        @pl.when(epoch < me)
+        def _(epoch=epoch):
+            send_image(epoch)
+            coded(epoch, me).start()
+
     def offer(step):
         @pl.when(me + step < n_epoch)
         def _(epoch=me + step):
@@ -765,11 +766,9 @@
 
         @pl.when(me == 0)
         def _():
-            wait_small(1)
             lay_tiles()
-            theirs(1)
             first()
-            answer(1)
+            host(1)
             offer(3)
             wait_small(2)
             wait_image(1)
@@ -778,8 +777,8 @@
             answer(2)
             host(3)
             wait_image(3)
+            wait_image(2)
             ours(3)
-            wait_image(2)
             ours(2)
 
         @pl.when(me > 0)
@@ -791,7 +790,7 @@
             for step in range(2, 0, -1):
                 mine(step)
 
-        for step in range(1, n_epoch):
+        for step in (1, 3, 2):
             finish(step)
     else:
         lay_tiles()
@@ -813,7 +812,7 @@
         rest = pl.ds(0, n_epoch - 1)
 
         def drain(source, kind, u, s):
-            copy(source, source, send_sem.at[kind], recv_sem.at[0, kind], device(me, u, s)).wait_send()
+            copy(source, source, send_sem.at[kind], recv_sem.at[0, 0], device(me, u, s)).wait_send()
 
         for number in range(1, n_epoch):
 
@@ -931,7 +930,7 @@
             pltpu.VMEM(template.shape, f32),
             dma((9,)),
             dma((n_image + 5,)),
-            dma((max(n_epoch - 1, 1), n_image + 5)),
+            dma((max(n_epoch - 1, 1), n_image + 4)),
             dma((n_image,)),
             dma((n_image,)),
             pltpu.SemaphoreType.REGULAR((n_epoch,)),

time: 12.9 us -> 12.8 us (level)
  no operation moved by 1% of the time
where the time goes in v8:
time: 12.8 us; the launch traced here: 12.6 us
  Pallas kernels  12 us (94%)
  between operations  0.64 us (5%)
    pallas_call x1, Pallas kernels, local(): pl.pallas_call(functools.partial(kernel, sizes), out_shape=(pltpu.VMEM(sc...  11.3 us
    pallas_call x1, Pallas kernels, local(): pl.pallas_call(leave, out_shape=(jax.ShapeDtypeStruct(science.shape, f32)...  0.7 us

profile of v8, /device:TPU:0, one launch (start us, length us, event | category | flops | bytes accessed | tf_op | source)
XLA Modules:
  0.0 12.6 jit_solution(3712233946565213412)
XLA Ops:
  0.6 11.3 %shard_map.104 = (f32[4,24,256]{2,1,0:T(8,128)S(1)}, f32[2,24,256]{2,1,0:T(8,128)S(1)}) custom-call(s32[16]{0:T(128)} %intersection_hbm.1, s32[2,4]{1,0:T(2,128)} %bitcast.5, s32[4,16]{1,0:T(4,128)} %basis_index_hbm.1, f32[6,4,16]{2,1,0:T(4,128)} %bitcast.4, bf16[2,24,256]{2,1,0:T(8,128)(2,1)} %template_hbm.1, f32[4,24,256]{2,1,0:T(8,128)} %science_hbm.1, ...), custom_call_target="tpu_custom_call" | custom-call | tf_op jit(solution)/shard_map/pallas_call | solution.py:883
  11.9 0.7 %shard_map.105 = (f32[4,24,256]{2,1,0:T(8,128)}, f32[2,24,256]{2,1,0:T(8,128)}) custom-call(f32[4,24,256]{2,1,0:T(8,128)S(1)} %get-tuple-element.4.residual, f32[2,24,256]{2,1,0:T(8,128)S(1)} %get-tuple-element.5.coadd), custom_call_target="tpu_custom_call" | custom-call | tf_op jit(solution)/shard_map/pallas_call | solution.py:945

commit v9 on v8

--- a/solution.py
+++ b/solution.py
@@ -178,6 +178,8 @@
             return strip + u[0] < strip
         return band + s[0] < band
 
+    swap = n_epoch == 4
+
     barrier = pltpu.get_barrier_semaphore()
 
     def signal(sem, epoch, u, s):
@@ -206,7 +208,13 @@
             lambda u=u, s=s: signal(token.at[me], me, u, s),
         )
     for epoch in range(n_epoch - 1):
-        pl.when(epoch < me)(lambda epoch=epoch: signal(token.at[me], epoch, none, none))
+        if swap and epoch == 0:
+            pl.when(me == n_epoch - 1)(lambda: to_epoch(token.at[me], 0))
+            pl.when(jnp.logical_and(me > 0, me < n_epoch - 1))(
+                lambda: signal(token.at[me], 0, none, none)
+            )
+        else:
+            pl.when(epoch < me)(lambda epoch=epoch: signal(token.at[me], epoch, none, none))
 
     def slot_of(sender, receiver):
         return sender - (sender > receiver).astype(jnp.int32)
@@ -666,9 +674,12 @@
     def offer(step):
         @pl.when(me + step < n_epoch)
         def _(epoch=me + step):
-            pl.semaphore_wait(token.at[epoch], 1)
+            far = swap and step == n_epoch - 1
+            pl.semaphore_wait(token.at[epoch], partners if far else 1)
             send_small(epoch)
             coefficient_tile(epoch, me).start()
+            if far:
+                send_image(epoch)
             coded(epoch, me).start()
 
     early = n_epoch - 2 if n_epoch == 4 else n_epoch - 1
@@ -749,7 +760,10 @@
 
     def finish(step):
         gather(step)
-        pl.when(partner(step) < me)(lambda: settle(step))
+        back = partner(step) < me
+        if swap:
+            back = jnp.logical_and(back, me - partner(step) < n_epoch - 1)
+        pl.when(back)(lambda: settle(step))
 
     def gather(step):
         epoch = partner(step)
@@ -775,10 +789,11 @@
             theirs(2)
             ours(1)
             answer(2)
-            host(3)
+            wait_small(3)
+            theirs(3)
             wait_image(3)
+            ours(3)
             wait_image(2)
-            ours(3)
             ours(2)
 
         @pl.when(me > 0)
@@ -790,6 +805,12 @@
             for step in range(2, 0, -1):
                 mine(step)
 
+            @pl.when(me == n_epoch - 1)
+            def _():
+                wait_image(0)
+                ours(3)
+
+
         for step in (1, 3, 2):
             finish(step)
     else:
@@ -814,11 +835,11 @@
         def drain(source, kind, u, s):
             copy(source, source, send_sem.at[kind], recv_sem.at[0, 0], device(me, u, s)).wait_send()
 
-        for number in range(1, n_epoch):
-
-            @pl.when(me == number)
+        for number in range(n_epoch):
+
+            @pl.when(jnp.logical_and(me == number, number > 0 or swap))
             def _(number=number):
-                lead = pl.ds(0, number)
+                lead = pl.ds(0, max(number, 1))
                 for u, s, kind in images:
                     if u is none and s is none:
                         source = chosen.at[lead]
@@ -833,9 +854,14 @@
                         lambda u=u, s=s, kind=kind, source=source: drain(source, kind, u, s),
                     )
 
-            @pl.when(me == n_epoch - 1 - number)
-            def _(number=number):
-                drain(model_out.at[pl.ds(0, number)], MODEL, none, none)
+            models_sent = n_epoch - 1 - number
+            if swap and number == 0:
+                models_sent -= 1
+            if models_sent > 0:
+
+                @pl.when(me == number)
+                def _(models_sent=models_sent):
+                    drain(model_out.at[pl.ds(0, models_sent)], MODEL, none, none)
 
         for held, kind in (
             (offsets_in, OFFS),

time: 12.8 us -> 12.5 us (0.977)
  Pallas kernels: 12 us -> 11.7 us
    pallas_call x1, Pallas kernels: 11.3 us -> 11 us  [local(): pl.pallas_call(functools.partial(kernel, sizes), out_shape=(pltpu.VMEM(sc...]
where the time goes in v9:
time: 12.5 us; the launch traced here: 12.4 us
  Pallas kernels  11.7 us (94%)
  between operations  0.64 us (5%)
    pallas_call x1, Pallas kernels, local(): pl.pallas_call(functools.partial(kernel, sizes), out_shape=(pltpu.VMEM(sc...  11 us
    pallas_call x1, Pallas kernels, local(): pl.pallas_call(leave, out_shape=(jax.ShapeDtypeStruct(science.shape, f32)...  0.7 us

profile of v9, /device:TPU:0, one launch (start us, length us, event | category | flops | bytes accessed | tf_op | source)
XLA Modules:
  0.0 12.4 jit_solution(13882747452315076244)
XLA Ops:
  0.6 11.0 %shard_map.104 = (f32[4,24,256]{2,1,0:T(8,128)S(1)}, f32[2,24,256]{2,1,0:T(8,128)S(1)}) custom-call(s32[16]{0:T(128)} %intersection_hbm.1, s32[2,4]{1,0:T(2,128)} %bitcast.5, s32[4,16]{1,0:T(4,128)} %basis_index_hbm.1, f32[6,4,16]{2,1,0:T(4,128)} %bitcast.4, bf16[2,24,256]{2,1,0:T(8,128)(2,1)} %template_hbm.1, f32[4,24,256]{2,1,0:T(8,128)} %science_hbm.1, ...), custom_call_target="tpu_custom_call" | custom-call | tf_op jit(solution)/shard_map/pallas_call | solution.py:909
  11.7 0.7 %shard_map.105 = (f32[4,24,256]{2,1,0:T(8,128)}, f32[2,24,256]{2,1,0:T(8,128)}) custom-call(f32[4,24,256]{2,1,0:T(8,128)S(1)} %get-tuple-element.4.residual, f32[2,24,256]{2,1,0:T(8,128)S(1)} %get-tuple-element.5.coadd), custom_call_target="tpu_custom_call" | custom-call | tf_op jit(solution)/shard_map/pallas_call | solution.py:971

commit v10 on v9

--- a/solution.py
+++ b/solution.py
@@ -300,7 +300,7 @@
         images_in.append((a, b, kind))
 
     def send_image(epoch):
-        for u, s, kind in images:
+        for u, s, kind in reversed(images):
             guarded(
                 both(u[3], s[3]), lambda u=u, s=s, kind=kind: image(epoch, u, s, kind, me).start()
             )
@@ -792,8 +792,8 @@
             wait_small(3)
             theirs(3)
             wait_image(3)
+            wait_image(2)
             ours(3)
-            wait_image(2)
             ours(2)
 
         @pl.when(me > 0)

time: 12.5 us -> 12.4 us (level)
  no operation moved by 1% of the time
where the time goes in v10:
time: 12.4 us; the launch traced here: 12.3 us
  Pallas kernels  11.6 us (94%)
  between operations  0.64 us (5%)
    pallas_call x1, Pallas kernels, local(): pl.pallas_call(functools.partial(kernel, sizes), out_shape=(pltpu.VMEM(sc...  10.9 us
    pallas_call x1, Pallas kernels, local(): pl.pallas_call(leave, out_shape=(jax.ShapeDtypeStruct(science.shape, f32)...  0.7 us

profile of v10, /device:TPU:0, one launch (start us, length us, event | category | flops | bytes accessed | tf_op | source)
XLA Modules:
  0.0 12.3 jit_solution(16549547249419894553)
XLA Ops:
  0.6 10.9 %shard_map.104 = (f32[4,24,256]{2,1,0:T(8,128)S(1)}, f32[2,24,256]{2,1,0:T(8,128)S(1)}) custom-call(s32[16]{0:T(128)} %intersection_hbm.1, s32[2,4]{1,0:T(2,128)} %bitcast.5, s32[4,16]{1,0:T(4,128)} %basis_index_hbm.1, f32[6,4,16]{2,1,0:T(4,128)} %bitcast.4, bf16[2,24,256]{2,1,0:T(8,128)(2,1)} %template_hbm.1, f32[4,24,256]{2,1,0:T(8,128)} %science_hbm.1, ...), custom_call_target="tpu_custom_call" | custom-call | tf_op jit(solution)/shard_map/pallas_call | solution.py:909
  11.6 0.7 %shard_map.105 = (f32[4,24,256]{2,1,0:T(8,128)}, f32[2,24,256]{2,1,0:T(8,128)}) custom-call(f32[4,24,256]{2,1,0:T(8,128)S(1)} %get-tuple-element.4.residual, f32[2,24,256]{2,1,0:T(8,128)S(1)} %get-tuple-element.5.coadd), custom_call_target="tpu_custom_call" | custom-call | tf_op jit(solution)/shard_map/pallas_call | solution.py:971
